TPU v7x, 128 devices: a whole 4x4x4 slice. The times are simulated.
128 devices in a mesh: grp: 4 (over y), slab: 32 (over x, z, core).
Axes of the slice: x: 4, y: 4, z: 4, core: 2. Of those that a mesh axis runs over, the one named last changes fastest.
Arguments:
- state: float32 [4, 2, 256, 128, 256], P(None, None, 'grp', 'slab'), may hold values from -5.6 to 5.6
- kz_group: int32 [256], replicated, may hold values from 0 to 7, as said below
- cutoffs: int32 [3], replicated, may hold values from 28 to 32
- damping: float32 [8], replicated, may hold values from 0.005 to 0.5
- power: float32 [8], replicated, may hold values from 0.2 to 4
Outputs:
- new_state: float32 [4, 2, 256, 128, 256], P(None, None, 'grp', 'slab')
Inputs may be any that keep to these rules, and one draw needn't show every extreme that they name: `kz_group`: each of the 8 groups holds exactly 32 indices.
All inputs are finite; a program needn't handle non-finite values.
Results may differ from a plain program's by a relative error of at most 0.00005.
Values sent between devices are 32-bit elements; how exact they have to be, the bound alone decides.
No kernel may reach another device: no remote copies, remote signals or barrier semaphores. Data moves between devices by JAX's collectives and lax.ppermute only.
A program may use at most 128 MiB of HBM per device.

v0:
```python
import functools
import math

import jax
import jax.numpy as jnp
import numpy as np
from jax import lax
from jax.experimental import pallas as pl
from jax.experimental.pallas import tpu as pltpu
from jax.sharding import Mesh
from jax.sharding import PartitionSpec as P

N = 256
GROUPS = 8
KX = 128
GMODES = 32
KEPT_COLS = 88
SLAB = ("slab_0", "slab_1", "slab_2")
ALL = ("grp",) + SLAB

TWO_PI = 6.283185307179586
WAVE = TWO_PI / N
TIME_STEP = 0.25
CORIOLIS = 1.0
BRUNT_SQUARED = 2.0
EPSILON = 1e-06
SCALE = 1.0 / 4096.0
FIELDS_OUT = 6
FIELDS_BACK = 5
ROWS_OUT = 8 * FIELDS_OUT
ROWS_BACK = 8 * FIELDS_BACK

F32 = jnp.float32
BF16 = jnp.bfloat16


def halves(table):
    high = table.astype(np.float32).astype(jnp.bfloat16)
    low = (table - high.astype(np.float64)).astype(np.float32).astype(jnp.bfloat16)
    return jnp.asarray(high), jnp.asarray(low)


def angle(rows, cols):
    return 2.0 * np.pi / N * (np.outer(rows, cols) % N).astype(np.float64)


def signed(index):
    return np.where(index < N // 2, index, index - N)


def tables():
    points = np.arange(N)
    theta = angle(points, points)
    cosine, sine = np.cos(theta), np.sin(theta)
    wave = (WAVE * signed(points))[None, :]
    y_inverse = np.concatenate([cosine, sine, wave * cosine, wave * sine], axis=0)
    z_table = np.concatenate([cosine, sine], axis=1)
    weight = np.where(np.arange(KX) == 0, 1.0, 2.0) * SCALE
    x_inverse = np.concatenate([cosine[:, :KX] * weight, -sine[:, :KX] * weight], axis=1)
    x_forward = np.concatenate([cosine[:KEPT_COLS], -sine[:KEPT_COLS]], axis=0) * SCALE
    y_forward = np.concatenate([cosine, sine], axis=1)
    return [halves(t) for t in (y_inverse, z_table, x_inverse, x_forward, y_forward)]


def split(value):
    high = value.astype(BF16)
    low = (value - high.astype(F32)).astype(BF16)
    return high, low


def product(left, right, dims):
    def one(a, b):
        return lax.dot_general(a, b, (dims, ((), ())), preferred_element_type=F32)

    return one(left[0], right[0]) + (one(left[0], right[1]) + one(left[1], right[0]))


def slot_rows(group_row, slots):
    member = (lax.broadcasted_iota(jnp.int32, (GROUPS, N), 0) == group_row).astype(F32)
    earlier = (
        lax.broadcasted_iota(jnp.int32, (N, N), 0) < lax.broadcasted_iota(jnp.int32, (N, N), 1)
    ).astype(F32)
    count = jnp.dot(member.astype(BF16), earlier.astype(BF16), preferred_element_type=F32)
    first = (GMODES * lax.broadcasted_iota(jnp.int32, (GROUPS, N), 0)).astype(F32)
    place = jnp.sum(member * (first + count), axis=0, keepdims=True).astype(jnp.int32)
    return slots == place


def signed_row(shape):
    index = lax.broadcasted_iota(jnp.int32, shape, len(shape) - 1)
    return jnp.where(index < N // 2, index, index - N)


def send_kernel(state, w_high, w_low, sent, sums):
    sign = jnp.where(lax.broadcasted_iota(jnp.int32, (N, 128), 1) < 64, -1.0, 1.0).astype(F32)
    flux = jnp.zeros((128, N), F32)
    energy = jnp.zeros((128, N), F32)
    for x in range(4):
        flow_x, flow_y, flow_z, buoyant = (state[f * 4 + x] for f in range(4))
        flux = flux + flow_z * buoyant
        energy = energy + 0.5 * (
            flow_x * flow_x
            + flow_y * flow_y
            + flow_z * flow_z
            + buoyant * buoyant * (1.0 / BRUNT_SQUARED)
        )
    group = (lax.broadcasted_iota(jnp.int32, (128, N), 0) // GMODES) % 2
    parts = []
    for value in (flux, energy):
        for which in range(2):
            parts.append(jnp.sum(jnp.where(group == which, value, 0.0)))
    line = lax.broadcasted_iota(jnp.int32, (8, 128), 0)
    total = jnp.zeros((8, 128), F32)
    for k, part in enumerate(parts):
        total = jnp.where(line == k, part, total)
    sums[...] = total

    def put(slot, x, value):
        for low in range(2):
            start = slot * 8 + low * 4 + x
            sent[pl.ds(start, 128, stride=ROWS_OUT), :] = value[low * 128 : (low + 1) * 128]

    for f in range(4):
        derived = {0: 4, 2: 5}.get(f)
        rows = 1024 if derived else 512
        for pair in range(2):
            first = f * 4 + pair * 2
            piece = state[first : first + 2].reshape(256, N)
            made = product((w_high[:rows], w_low[:rows]), split(piece), ((1,), (1,)))
            for k in range(2):
                x = pair * 2 + k
                cos_part = made[0:256, k * 128 : (k + 1) * 128]
                sin_part = made[256:512, k * 128 : (k + 1) * 128]
                put(f, x, cos_part + sign * pltpu.roll(sin_part, 64, 1))
                if derived:
                    cos_part = made[512:768, k * 128 : (k + 1) * 128]
                    sin_part = made[768:1024, k * 128 : (k + 1) * 128]
                    put(derived, x, sign * pltpu.roll(cos_part, 64, 1) - sin_part)


def grid_kernel(
    came,
    groups,
    zt_high,
    zt_low,
    xi_high,
    xi_low,
    xf_high,
    xf_low,
    sent,
    wz_high,
    wz_low,
    rows_z,
    planes,
    lines,
):
    index = lax.broadcasted_iota(jnp.int32, (512, N), 0)
    picked = slot_rows(groups[0:1, :], (index // 128) * 64 + index % 64).astype(BF16)
    is_real = (lax.broadcasted_iota(jnp.int32, (512, 512), 0) % 128) < 64
    for table, out in ((zt_high, wz_high), (zt_low, wz_low)):
        moved = jnp.dot(picked, table[...], preferred_element_type=F32)
        turned = jnp.concatenate([-moved[:, N:], moved[:, :N]], axis=1)
        out[...] = jnp.where(is_real, moved, turned).astype(BF16)
    kz = lax.dot_general(
        signed_row((8, N)).astype(F32).astype(BF16),
        picked,
        (((1,), (1,)), ((), ())),
        preferred_element_type=F32,
    )
    kz = kz[0:1, :] * WAVE
    lane = lax.broadcasted_iota(jnp.int32, (1, 512), 1)
    kz_turn = jnp.where(lane % 128 < 64, kz, -kz)
    turn = jnp.where(lane % 128 < 64, 1.0, -1.0).astype(F32)
    kx = (lax.broadcasted_iota(jnp.int32, (256, 1), 0) % 128).astype(F32) * WAVE

    upper = lax.broadcasted_iota(jnp.int32, (16, 8, 128), 1) < 4

    def field(f):
        pieces = []
        for g in range(4):
            tiles = came[g * 32 : (g + 1) * 32, f * 8 : (f + 1) * 8, :].reshape(16, 2, 8, 128)
            even, odd = tiles[:, 0], tiles[:, 1]
            first = jnp.where(upper, even, pltpu.roll(odd, 4, 1))
            second = jnp.where(upper, pltpu.roll(even, 4, 1), odd)
            pieces.append(
                jnp.concatenate([first.reshape(128, 128), second.reshape(128, 128)], axis=0)
            )
        return jnp.concatenate(pieces, axis=1)

    def turned(value):
        return jnp.concatenate(
            [pltpu.roll(value[:, g * 128 : (g + 1) * 128], 64, 1) for g in range(4)], axis=1
        )

    weights = (wz_high[...], wz_low[...])

    def vertical(value, slot):
        made = product(split(value), weights, ((1,), (0,)))
        for plane in range(2):
            part = made[plane * 128 : (plane + 1) * 128]
            rows_z[slot, 0:128, plane * N : (plane + 1) * N] = part[:, :N]
            rows_z[slot, 128:256, plane * N : (plane + 1) * N] = part[:, N:]

    flow_x = field(0)
    turned_x = turned(flow_x)
    vertical(flow_x, 0)
    flow_z = field(2)
    turned_z = turned(flow_z)
    vertical(flow_z, 2)
    vertical(kx * (turn * turned_z) - kz_turn * turned_x, 5)
    flow_y = field(1)
    turned_y = turned(flow_y)
    vertical(flow_y, 1)
    vertical(field(5) + kz_turn * turned_y, 4)
    vertical(-(kx * (turn * turned_y)) - field(4), 6)
    vertical(field(3), 3)

    x_inverse = (xi_high[...], xi_low[...])
    for slot in range(7):
        planes[slot] = product(x_inverse, split(rows_z[slot]), ((1,), (0,)))

    x_forward = (xf_high[...], xf_low[...])

    def horizontal(value, slot):
        made = product(x_forward, split(value), ((1,), (0,)))
        for plane in range(2):
            low, high = plane * KEPT_COLS, (plane + 1) * KEPT_COLS
            lines[slot, low:high, 0:N] = made[0:KEPT_COLS, plane * N : (plane + 1) * N]
            lines[slot, low:high, N:] = made[KEPT_COLS:, plane * N : (plane + 1) * N]

    u, v, w, b, ox, oy, oz = range(7)
    horizontal(planes[v] * planes[oz] - planes[w] * planes[oy], 0)
    horizontal(planes[w] * planes[ox] - planes[u] * planes[oz], 1)
    horizontal(planes[u] * planes[oy] - planes[v] * planes[ox], 2)
    horizontal(planes[u] * planes[b], 3)
    horizontal(planes[v] * planes[b], 4)
    horizontal(planes[w] * planes[b], 5)

    row = lax.broadcasted_iota(jnp.int32, (2 * KEPT_COLS, 1), 0)
    kx_kept = jnp.where(row < KEPT_COLS, row, row - KEPT_COLS).astype(F32) * WAVE
    upper_kept = lax.broadcasted_iota(jnp.int32, (11, 8, 128), 1) < 4

    def slots(value):
        return product(split(value), weights, ((1,), (1,)))

    def put(value, f):
        for g in range(4):
            part = value[:, g * 128 : (g + 1) * 128]
            first = part[:KEPT_COLS].reshape(11, 8, 128)
            second = part[KEPT_COLS:].reshape(11, 8, 128)
            even = jnp.where(upper_kept, first, pltpu.roll(second, 4, 1))
            odd = jnp.where(upper_kept, pltpu.roll(first, 4, 1), second)
            for j in range(11):
                sent[g * 32 + 2 * j, f * 8 : (f + 1) * 8, :] = even[j]
                sent[g * 32 + 2 * j + 1, f * 8 : (f + 1) * 8, :] = odd[j]

    for k in range(3):
        put(slots(lines[k]), k)
    put(slots(kx_kept * lines[3]) + kz * slots(lines[5]), 3)
    put(slots(lines[4]), 4)
    for g in range(4):
        sent[g * 32 + 22 : (g + 1) * 32] = jnp.zeros((10, ROWS_BACK, 128), F32)


def update_kernel(
    integers, reals, came, state, groups, yf_high, yf_low, made_state
):
    grp, slab = integers[0], integers[1]
    cut_x, cut_y, cut_z = integers[2], integers[3], integers[4]
    index = lax.broadcasted_iota(jnp.int32, (64, N), 0)
    picked = slot_rows(groups[0:1, :], index + grp * 64)
    mode_z = jnp.sum(jnp.where(picked, signed_row((64, N)), 0), axis=1, keepdims=True)
    mode_y = signed_row((1, N))
    slot = lax.broadcasted_iota(jnp.int32, (64, 1), 0)
    forcing = jnp.where(slot < GMODES, reals[0], reals[1])
    damping = jnp.where(slot < GMODES, reals[2], reals[3])
    wave_z = mode_z.astype(F32) * WAVE
    wave_y = mode_y.astype(F32) * WAVE
    kept_zy = (96 * jnp.abs(mode_z) <= cut_z * N) & (96 * jnp.abs(mode_y) <= cut_y * N)
    table = (yf_high[...], yf_low[...])
    wave_zy = wave_y * wave_y + wave_z * wave_z
    grown = 1.0 + TIME_STEP * forcing
    rotation = TIME_STEP * CORIOLIS
    for x in range(4):
        mode_x = slab * 4 + x
        wave_x = mode_x.astype(F32) * WAVE
        kept = kept_zy & (96 * mode_x <= cut_x * N)

        def spectral(f):
            pieces = [
                came[pl.ds(f * 8 + low * 4 + x, 128, stride=ROWS_BACK), :].T for low in range(2)
            ]
            got = product(split(jnp.concatenate(pieces, axis=1)), table, ((1,), (0,)))
            real = got[0:64, :N] + got[64:128, N:]
            imag = got[64:128, :N] - got[0:64, N:]
            return real, imag

        moments = [spectral(f) for f in range(3)]
        partial_b = spectral(3)
        flux_y = spectral(4)
        source = [partial_b[k] + wave_y * flux_y[k] for k in range(2)]
        sources = (source[1], -source[0])
        wave_sq = wave_x * wave_x + wave_zy
        implicit = 1.0 + TIME_STEP * damping * wave_sq
        square = implicit * implicit
        first = 1.0 / (square + rotation * rotation)
        second = 1.0 / (square + TIME_STEP * TIME_STEP * BRUNT_SQUARED)
        inverse_sq = 1.0 / jnp.where(wave_sq == 0, 1.0, wave_sq)
        for k in range(2):
            rows = slice(k * 64, (k + 1) * 64)
            flows = [state[f * 4 + x, rows, :] for f in range(4)]
            right = [
                flows[f] * grown + jnp.where(kept, TIME_STEP * moments[f][k], 0.0)
                for f in range(3)
            ]
            right_b = flows[3] + jnp.where(kept, TIME_STEP * sources[k], 0.0)
            new_x = (implicit * right[0] + rotation * right[1]) * first
            new_y = (implicit * right[1] - rotation * right[0]) * first
            new_z = (implicit * right[2] + TIME_STEP * right_b) * second
            new_b = (implicit * right_b - TIME_STEP * BRUNT_SQUARED * right[2]) * second
            inner = (wave_x * new_x + wave_y * new_y + wave_z * new_z) * inverse_sq
            made_state[x, rows, :] = new_x - wave_x * inner
            made_state[4 + x, rows, :] = new_y - wave_y * inner
            made_state[8 + x, rows, :] = new_z - wave_z * inner
            made_state[12 + x, rows, :] = new_b


VM = pl.BlockSpec(memory_space=pltpu.VMEM)
SM = pl.BlockSpec(memory_space=pltpu.SMEM)


def shards(state, kz_group, cutoffs, damping, power):
    grp = lax.axis_index("grp")
    slab = lax.axis_index(SLAB)
    y_inverse, z_table, x_inverse, x_forward, y_forward = tables()
    groups = jnp.broadcast_to(kz_group[None, :], (8, N))
    rows = state.transpose(0, 3, 1, 2, 4).reshape(16, 128, N)

    sent, sums = pl.pallas_call(
        send_kernel,
        out_shape=(
            jax.ShapeDtypeStruct((128 * ROWS_OUT, 128), F32),
            jax.ShapeDtypeStruct((8, 128), F32),
        ),
        in_specs=[VM] * 3,
        out_specs=(VM, VM),
        name="send",
    )(rows, *y_inverse)
    came = lax.all_to_all(sent.reshape(128, ROWS_OUT, 128), ALL, 0, 0, tiled=True)
    for axis in SLAB:
        sums = lax.psum(sums, axis)

    back = pl.pallas_call(
        grid_kernel,
        out_shape=jax.ShapeDtypeStruct((128, ROWS_BACK, 128), F32),
        in_specs=[VM] * 8,
        out_specs=VM,
        scratch_shapes=[
            pltpu.VMEM((512, 512), BF16),
            pltpu.VMEM((512, 512), BF16),
            pltpu.VMEM((7, 256, 512), F32),
            pltpu.VMEM((7, 256, 512), F32),
            pltpu.VMEM((6, 2 * KEPT_COLS, 512), F32),
        ],
        name="grid",
    )(came, groups, *z_table, *x_inverse, *x_forward)
    came = lax.all_to_all(back, ALL, 0, 0, tiled=True)

    means = sums[:4, 0] / (GMODES * KX * N)
    power_here = lax.dynamic_slice_in_dim(power, grp * 2, 2)
    damping_here = lax.dynamic_slice_in_dim(damping, grp * 2, 2)
    forcing = (power_here - means[:2]) / (2.0 * (means[2:] + EPSILON))
    reals = jnp.concatenate([forcing, damping_here])
    integers = jnp.concatenate([jnp.stack([grp, slab]).astype(jnp.int32), cutoffs])
    made = pl.pallas_call(
        update_kernel,
        out_shape=jax.ShapeDtypeStruct((16, 128, N), F32),
        in_specs=[SM, SM] + [VM] * 5,
        out_specs=VM,
        name="update",
    )(integers, reals, came.reshape(128 * ROWS_BACK, 128), rows, groups, *y_forward)
    return made.reshape(4, 4, 2, 64, N).transpose(0, 2, 3, 1, 4)


def solution(mesh):
    finer = Mesh(
        mesh.devices.reshape(mesh.shape["grp"], 4, 4, 2), ("grp", "slab_0", "slab_1", "slab_2")
    )
    return jax.shard_map(
        shards,
        mesh=finer,
        in_specs=(P(None, None, "grp", SLAB, None), P(), P(), P(), P()),
        out_specs=P(None, None, "grp", SLAB, None),
        check_vma=False,
    )
```

profile of v0, /device:TPU:0, one launch (start us, length us, event | category | flops | bytes accessed | tf_op | source)
XLA Modules:
  0.0 142.4 jit_solution(2369251021166377719)
XLA Ops:
  0.0 3.3 %copy.18 = f32[4,4,2,64,256]{4,3,2,1,0:T(8,128)} copy(f32[4,4,2,64,256]{4,1,3,2,0:T(4,128)} %bitcast.15) | data formatting | bytes 4194304 | tf_op jit(solution)/shard_map/transpose | solution.py:337
  3.3 6.8 %send.1 = (f32[6144,128]{1,0:T(8,128)}, f32[8,128]{1,0:T(8,128)}) custom-call(f32[16,128,256]{2,1,0:T(8,128)} %bitcast.10, bf16[1024,256]{1,0:T(8,128)(2,1)} %constant.44.clone.w_high, bf16[1024,256]{1,0:T(8,128)(2,1)} %constant.45.clone.w_low), custom_call_target="tpu_custom_call" | custom-call | tf_op jit(solution)/shard_map/send/pallas_call | solution.py:339
  10.1 0.0 copy-start.2
  10.1 53.0 %all_to_all.10.came = f32[128,48,128]{2,1,0:T(8,128)} all-to-all(f32[128,48,128]{2,1,0:T(8,128)} %bitcast.14), channel_id=1, replica_groups=mesh['grp'=4,'slab_0'=4,'slab_1'=4,'slab_2'=2] {'grp','slab_0','slab_1',..., dimensions={0} | all-to-all | bytes 6291456 | tf_op jit(solution)/shard_map/all_to_all | solution.py:349
  63.0 0.0 copy-done.2
  63.0 0.6 broadcast_in_dim.2.groups
  63.6 13.2 %grid.1 = f32[128,40,128]{2,1,0:T(8,128)} custom-call(f32[128,48,128]{2,1,0:T(8,128)} %all_to_all.10.came, s32[8,256]{1,0:T(8,128)} %broadcast_in_dim.2.groups, bf16[256,512]{1,0:T(8,128)(2,1)} %constant.46.clone.zt_high.yf_high, bf16[256,512]{1,0:T(8,128)(2,1)} %constant.47.clone.zt_low.yf_low, bf16[256,256]{1,0:T(8,128)(2,1)} %constant.48.clone.xi_high, ...), custom_call_target="tpu_custom_call" | custom-call | tf_op jit(solution)/shard_map/grid/pallas_call | solution.py:353
  76.9 0.0 copy-start.5
  76.9 0.0 copy-start.1
  76.9 0.0 copy-start.3
  76.9 0.0 copy-start.4
  76.9 4.8 %all-to-all-start.1 = ((f32[128,40,128]{2,1,0:T(8,128)}), f32[128,40,128]{2,1,0:T(8,128)S(1)}, u32[]{:S(2)}, u32[]{:S(2)}) async-start(f32[128,40,128]{2,1,0:T(8,128)} %grid.1), calls=%async_computation.1 | async-start | bytes 5242880 | tf_op jit(solution)/shard_map/all_to_all | solution.py:367
  81.7 0.0 copy-done.5
  81.7 0.1 dynamic_slice.7
  81.8 0.0 copy-done.1
  81.8 32.9 %psum.21 = f32[8,128]{1,0:T(8,128)S(1)} all-reduce(f32[8,128]{1,0:T(8,128)S(1)} %copy-done.1), channel_id=1, replica_groups=mesh['grp'=4,'slab_0'=4,'slab_1'=4,'slab_2'=2] {'slab_0'}, use_global_device_ids=true, to_apply=%region_0.0 | all-reduce | flops 1024 | bytes 8192 | tf_op jit(solution)/shard_map/psum | solution.py:351
  114.7 11.2 %psum.22 = f32[8,128]{1,0:T(8,128)S(1)} all-reduce(f32[8,128]{1,0:T(8,128)S(1)} %psum.21), channel_id=1, replica_groups=mesh['grp'=4,'slab_0'=4,'slab_1'=4,'slab_2'=2] {'slab_1'}, use_global_device_ids=true, to_apply=%region_1.0 | all-reduce | flops 1024 | bytes 8192 | tf_op jit(solution)/shard_map/psum | solution.py:351
  125.9 2.6 %psum.23 = f32[8,128]{1,0:T(8,128)S(1)} all-reduce(f32[8,128]{1,0:T(8,128)S(1)} %psum.22), channel_id=1, replica_groups=mesh['grp'=4,'slab_0'=4,'slab_1'=4,'slab_2'=2] {'slab_2'}, use_global_device_ids=true, to_apply=%region_2.0 | all-reduce | flops 1024 | bytes 8192 | tf_op jit(solution)/shard_map/psum | solution.py:351
  128.6 0.1 slice_reduce_fusion
  128.7 0.0 copy-done.3
  128.7 0.1 subtract_divide_fusion
  128.8 0.6 pad_maximum_fusion.reals
  129.5 0.0 copy-done.4
  129.5 0.6 pad_add_fusion.integers
  130.0 0.0 all-to-all-done.1
  130.1 0.0 copy-start
  130.1 1.5 %copy-done = f32[128,40,128]{2,1,0:T(8,128)} copy-done((f32[128,40,128]{2,1,0:T(8,128)}, f32[128,40,128]{2,1,0:T(8,128)S(1)}, u32[]{:S(2)}) %copy-start) | copy-done | bytes 2621464
  131.6 6.6 %update.1 = f32[16,128,256]{2,1,0:T(8,128)} custom-call(s32[5]{0:T(128)} %pad_add_fusion.integers, f32[4]{0:T(128)} %pad_maximum_fusion.reals, f32[5120,128]{1,0:T(8,128)} %bitcast.12, f32[16,128,256]{2,1,0:T(8,128)} %bitcast.11, s32[8,256]{1,0:T(8,128)} %broadcast_in_dim.2.groups, bf16[256,512]{1,0:T(8,128)(2,1)} %constant.46.clone.zt_high.yf_high, ...), custom_call_target="tpu_custom_call" | custom-call | tf_op jit(solution)/shard_map/update/pallas_call | solution.py:375
  138.2 4.3 %copy.21 = f32[4,4,2,64,256]{4,1,3,2,0:T(4,128)} copy(f32[4,4,2,64,256]{4,3,2,1,0:T(8,128)} %bitcast.13) | data formatting | bytes 4194304 | tf_op jit(solution)/shard_map/reshape | solution.py:382
  (1 shorter events, 0.0 us)
Async XLA Ops:
  10.1 53.0 %copy-start.2 = (s32[256]{0:T(256)S(1)}, s32[256]{0:T(256)}, u32[]{:S(2)}) copy-start(s32[256]{0:T(256)} %param.16) | copy-start | bytes 3076
  76.9 4.9 %copy-start.5 = (f32[8]{0:T(128)S(1)}, f32[8]{0:T(128)}, u32[]{:S(2)}) copy-start(f32[8]{0:T(128)} %param.18) | copy-start | bytes 100
  76.9 4.9 %copy-start.1 = (f32[8,128]{1,0:T(8,128)S(1)}, f32[8,128]{1,0:T(8,128)}, u32[]{:S(2)}) copy-start(f32[8,128]{1,0:T(8,128)} %get-tuple-element.7) | copy-start | bytes 12292
  76.9 51.8 %copy-start.3 = (f32[8]{0:T(128)S(1)}, f32[8]{0:T(128)}, u32[]{:S(2)}) copy-start(f32[8]{0:T(128)} %param.19) | copy-start | bytes 100
  76.9 52.6 %copy-start.4 = (s32[3]{0:T(128)S(1)}, s32[3]{0:T(128)}, u32[]{:S(2)}) copy-start(s32[3]{0:T(128)} %param.17) | copy-start | bytes 40
  76.9 53.2 %all-to-all-start.1 = ((f32[128,40,128]{2,1,0:T(8,128)}), f32[128,40,128]{2,1,0:T(8,128)S(1)}, u32[]{:S(2)}, u32[]{:S(2)}) async-start(f32[128,40,128]{2,1,0:T(8,128)} %grid.1), calls=%async_computation.1 | async-start | bytes 5242880 | tf_op jit(solution)/shard_map/all_to_all | solution.py:367
  130.1 1.5 %copy-start = (f32[128,40,128]{2,1,0:T(8,128)}, f32[128,40,128]{2,1,0:T(8,128)S(1)}, u32[]{:S(2)}) copy-start(f32[128,40,128]{2,1,0:T(8,128)S(1)} %all-to-all-done.1) | copy-start | bytes 7864324
where the time goes:
time: 144 us; the launch traced here: 142 us
  blocking collectives  99.7 us (69%)
  Pallas kernels  26.6 us (18%)
  local copies, waits for them, and re-layouts  9.74 us (7%)
  starting transfers between devices  4.81 us (3%)
  other arithmetic  1.46 us (1%)
    all_to_all x1, blocking collectives, shards(): lax.all_to_all(sent.reshape(128, ROWS_OUT, 128), ALL, 0, 0, tiled=True)  53 us
    psum x3, blocking collectives, shards(): sums = lax.psum(sums, axis)  46.8 us
    pallas_call x1, Pallas kernels, shards(): pl.pallas_call(grid_kernel, out_shape=jax.ShapeDtypeStruct((128, ROWS_BAC...  13.2 us
    pallas_call x1, Pallas kernels, shards(): pl.pallas_call(send_kernel, out_shape=(jax.ShapeDtypeStruct((128 * ROWS_O...  6.8 us
    pallas_call x1, Pallas kernels, shards(): pl.pallas_call(update_kernel, out_shape=jax.ShapeDtypeStruct((16, 128, N)...  6.6 us
    all_to_all x1, starting transfers between devices, shards(): came = lax.all_to_all(back, ALL, 0, 0, tiled=True)  4.81 us
    reshape x1, local copies, waits for them, and re-layouts, shards(): return made.reshape(4, 4, 2, 64, N).transpose(0, 2, 3, 1, 4)  4.26 us
    transpose x1, local copies, waits for them, and re-layouts, shards(): rows = state.transpose(0, 3, 1, 2, 4).reshape(16, 128, N)  3.28 us
  transfers between devices with their start and end apart: 1, of which 0 were waited for; matrix products, arithmetic and copies ran while one was open for 1% of the time, Pallas kernels for 0%

commit v1 on v0

v1 whole, which is shorter than its diff:
```python
import functools
import math

import jax
import jax.numpy as jnp
import numpy as np
from jax import lax
from jax.experimental import pallas as pl
from jax.experimental.pallas import tpu as pltpu
from jax.sharding import Mesh
from jax.sharding import PartitionSpec as P

N = 256
GROUPS = 8
KX = 128
GMODES = 32
KEPT_COLS = 88
SLAB = ("slab_0", "slab_1", "slab_2")
ALL = ("grp",) + SLAB
HALF = N // 2

TWO_PI = 6.283185307179586
WAVE = TWO_PI / N
TIME_STEP = 0.25
CORIOLIS = 1.0
BRUNT_SQUARED = 2.0
EPSILON = 1e-06
SCALE = 1.0 / 4096.0
FIELDS_OUT = 6
FIELDS_BACK = 5
ROWS_OUT = 8 * FIELDS_OUT
ROWS_BACK = 8 * FIELDS_BACK + 1

SEND_MIB = 24
GRID_MIB = 40
UPDATE_MIB = 24

F32 = jnp.float32
BF16 = jnp.bfloat16


def halves(table):
    high = table.astype(np.float32).astype(jnp.bfloat16)
    low = (table - high.astype(np.float64)).astype(np.float32).astype(jnp.bfloat16)
    return jnp.asarray(high), jnp.asarray(low)


def angle(rows, cols):
    return 2.0 * np.pi / N * (np.outer(rows, cols) % N).astype(np.float64)


def signed(index):
    return np.where(index < N // 2, index, index - N)


def folded():
    theta = angle(np.arange(HALF), np.arange(N))
    cosine, sine = np.cos(theta), np.sin(theta)
    odd = np.arange(N) % 2
    cosine[0], sine[0] = 1 - odd, odd
    return np.stack([cosine, sine])


def tables():
    points = np.arange(N)
    pair = folded()
    wave = (WAVE * signed(points))[None, None, :]
    y_inverse = np.concatenate([pair, wave * pair]).reshape(4 * HALF, N)
    fold = pair.reshape(N, N)
    theta = angle(points, np.arange(KX))
    weight = np.where(np.arange(KX) == 0, 1.0, 2.0) * SCALE
    x_inverse = np.concatenate([np.cos(theta) * weight, -np.sin(theta) * weight], axis=1)
    theta = theta.T[:KEPT_COLS]
    x_forward = np.concatenate([np.cos(theta), -np.sin(theta)], axis=0) * SCALE
    return [halves(t) for t in (y_inverse, fold.T.copy(), x_inverse, x_forward, fold)]


def split(value):
    high = value.astype(BF16)
    low = (value - high.astype(F32)).astype(BF16)
    return high, low


def product(left, right, dims):
    def one(a, b):
        return lax.dot_general(a, b, (dims, ((), ())), preferred_element_type=F32)

    return one(left[0], right[0]) + (one(left[0], right[1]) + one(left[1], right[0]))


def slot_rows(group_row, slots):
    member = (lax.broadcasted_iota(jnp.int32, (GROUPS, N), 0) == group_row).astype(F32)
    earlier = (
        lax.broadcasted_iota(jnp.int32, (N, N), 0) < lax.broadcasted_iota(jnp.int32, (N, N), 1)
    ).astype(F32)
    count = jnp.dot(member.astype(BF16), earlier.astype(BF16), preferred_element_type=F32)
    first = (GMODES * lax.broadcasted_iota(jnp.int32, (GROUPS, N), 0)).astype(F32)
    place = jnp.sum(member * (first + count), axis=0, keepdims=True).astype(jnp.int32)
    return slots == place


def signed_row(shape):
    index = lax.broadcasted_iota(jnp.int32, shape, len(shape) - 1)
    return jnp.where(index < N // 2, index, index - N)


def lanes(shape):
    return lax.broadcasted_iota(jnp.int32, shape, len(shape) - 1)


def send_kernel(state, w_high, w_low, sent, sums):
    sign = jnp.where(lanes((HALF, 128)) < 64, -1.0, 1.0).astype(F32)
    top = lax.broadcasted_iota(jnp.int32, (HALF, 128), 0) == 0
    flux = jnp.zeros((128, N), F32)
    energy = jnp.zeros((128, N), F32)

    def put(slot, x, even, odd):
        for low, value in ((0, even + odd), (1, even - odd)):
            sent[pl.ds(slot * 8 + low * 4 + x, 128, stride=ROWS_OUT), :] = value

    for pair in range(2):
        pieces = []
        for f in range(4):
            rows = []
            for x in (2 * pair, 2 * pair + 1):
                for part in range(2):
                    rows.append(
                        jnp.concatenate(
                            [
                                state[f * 2 + part, pl.ds(h * 4 + x, 64, stride=8), :]
                                for h in range(2)
                            ],
                            axis=1,
                        )
                    )
            pieces.append(jnp.concatenate(rows, axis=0))
        flow_x, flow_y, flow_z, buoyant = pieces
        moved = flow_z * buoyant
        held = 0.5 * (
            flow_x * flow_x
            + flow_y * flow_y
            + flow_z * flow_z
            + buoyant * buoyant * (1.0 / BRUNT_SQUARED)
        )
        flux = flux + (moved[:128] + moved[128:])
        energy = energy + (held[:128] + held[128:])
        for f in range(4):
            derived = {0: 4, 2: 5}.get(f)
            count = 512 if derived else 256
            made = product((w_high[:count], w_low[:count]), split(pieces[f]), ((1,), (1,)))
            for k in range(2):
                x = pair * 2 + k
                cols = slice(k * 128, (k + 1) * 128)
                even, odd = made[0:128, cols], made[128:256, cols]
                put(f, x, even, jnp.where(top, odd, sign * pltpu.roll(odd, 64, 1)))
                if derived:
                    even, odd = made[256:384, cols], made[384:512, cols]
                    even = sign * pltpu.roll(even, 64, 1)
                    put(derived, x, even, jnp.where(top, sign * pltpu.roll(odd, 64, 1), -odd))

    quarter = lanes((1, 128)) // 32
    total = jnp.zeros((1, 128), F32)
    for k, value in enumerate((flux, energy)):
        for which in range(2):
            low = which * GMODES
            part = jnp.sum(value[low : low + 32] + value[64 + low : 96 + low], axis=0, keepdims=True)
            part = part[:, :128] + part[:, 128:]
            part = part + pltpu.roll(part, 64, 1)
            part = part + pltpu.roll(part, 32, 1)
            total = jnp.where(quarter == 2 * k + which, part, total)
    sums[...] = jnp.broadcast_to(total, (8, 128))


def grid_kernel(
    came,
    sums,
    groups,
    zt_high,
    zt_low,
    xi_high,
    xi_low,
    xf_high,
    xf_low,
    sent,
    wz_high,
    wz_low,
    rows_z,
    planes,
    lines,
):
    picked = slot_rows(groups[...], lax.broadcasted_iota(jnp.int32, (N, N), 0)).astype(BF16)
    for table, out in ((zt_high, wz_high), (zt_low, wz_low)):
        out[...] = jnp.dot(picked, table[...], preferred_element_type=F32).astype(BF16)
    kz = lax.dot_general(
        signed_row((8, N)).astype(F32).astype(BF16),
        picked,
        (((1,), (1,)), ((), ())),
        preferred_element_type=F32,
    )
    kz = kz[0:1, :] * WAVE
    kx = (lax.broadcasted_iota(jnp.int32, (N, 1), 0) % 128).astype(F32) * WAVE
    weights = (wz_high[...], wz_low[...])

    def separate(first, second):
        low = lanes(first.shape) < 64
        return (
            jnp.where(low, first, pltpu.roll(second, 64, 1)),
            jnp.where(low, pltpu.roll(first, 64, 1), second),
        )

    upper = lax.broadcasted_iota(jnp.int32, (16, 8, 128), 1) < 4

    def field(f):
        pieces = []
        for g in range(4):
            tiles = came[g * 32 : (g + 1) * 32, f * 8 : (f + 1) * 8, :].reshape(16, 2, 8, 128)
            even, odd = tiles[:, 0], tiles[:, 1]
            first = jnp.where(upper, even, pltpu.roll(odd, 4, 1))
            second = jnp.where(upper, pltpu.roll(even, 4, 1), odd)
            pieces.append(
                jnp.concatenate([first.reshape(128, 128), second.reshape(128, 128)], axis=0)
            )
        near, far = separate(pieces[0], pieces[1]), separate(pieces[2], pieces[3])
        return tuple(jnp.concatenate([near[k], far[k]], axis=1) for k in range(2))

    start = lanes((N, HALF)) == 0

    def vertical(value, slot):
        made = product(split(jnp.concatenate(value, axis=0)), weights, ((1,), (0,)))
        even = (made[:N, :HALF], made[N:, :HALF])
        odd = (made[:N, HALF:], made[N:, HALF:])
        turned = (jnp.where(start, odd[0], -odd[1]), jnp.where(start, odd[1], odd[0]))
        for part in range(2):
            for k, both in enumerate((even[part] + turned[part], even[part] - turned[part])):
                for plane in range(2):
                    col = plane * N + k * HALF
                    rows_z[slot, part * 128 : (part + 1) * 128, col : col + HALF] = both[
                        plane * 128 : (plane + 1) * 128
                    ]

    flow_x = field(0)
    vertical(flow_x, 0)
    flow_z = field(2)
    vertical(flow_z, 2)
    vertical(
        (kx * flow_z[1] - kz * flow_x[1], kz * flow_x[0] - kx * flow_z[0]),
        5,
    )
    flow_y = field(1)
    vertical(flow_y, 1)
    slope = field(5)
    vertical((slope[0] + kz * flow_y[1], slope[1] - kz * flow_y[0]), 4)
    slope = field(4)
    vertical((-(kx * flow_y[1]) - slope[0], kx * flow_y[0] - slope[1]), 6)
    vertical(field(3), 3)

    x_inverse = (xi_high[...], xi_low[...])
    for slot in range(7):
        planes[slot] = product(x_inverse, split(rows_z[slot]), ((1,), (0,)))

    x_forward = (xf_high[...], xf_low[...])
    start_kept = lanes((KEPT_COLS, HALF)) == 0

    def horizontal(value, slot):
        pieces = []
        for plane in range(2):
            near = value[:, plane * N : plane * N + HALF]
            far = value[:, plane * N + HALF : (plane + 1) * N]
            pieces += [near + far, near - far]
        made = product(x_forward, split(jnp.concatenate(pieces, axis=1)), ((1,), (0,)))
        for plane in range(2):
            col = plane * N
            plus = made[:, col : col + HALF]
            odd_real = made[:KEPT_COLS, col + HALF : col + N]
            odd_imag = made[KEPT_COLS:, col + HALF : col + N]
            real, imag = plane * KEPT_COLS, (2 + plane) * KEPT_COLS
            lines[slot, real : real + KEPT_COLS, :HALF] = plus[:KEPT_COLS]
            lines[slot, imag : imag + KEPT_COLS, :HALF] = plus[KEPT_COLS:]
            lines[slot, real : real + KEPT_COLS, HALF:] = jnp.where(start_kept, odd_real, odd_imag)
            lines[slot, imag : imag + KEPT_COLS, HALF:] = jnp.where(
                start_kept, odd_imag, -odd_real
            )

    u, v, w, b, ox, oy, oz = range(7)
    horizontal(planes[v] * planes[oz] - planes[w] * planes[oy], 0)
    horizontal(planes[w] * planes[ox] - planes[u] * planes[oz], 1)
    horizontal(planes[u] * planes[oy] - planes[v] * planes[ox], 2)
    horizontal(planes[u] * planes[b], 3)
    horizontal(planes[v] * planes[b], 4)
    horizontal(planes[w] * planes[b], 5)

    row = lax.broadcasted_iota(jnp.int32, (4 * KEPT_COLS, 1), 0)
    kx_kept = (row % KEPT_COLS).astype(F32) * WAVE
    upper_kept = lax.broadcasted_iota(jnp.int32, (11, 8, 128), 1) < 4

    def slots(value):
        return product(split(value), weights, ((1,), (1,)))

    for g in range(4):
        low = (g * 32 + 22) * ROWS_BACK
        sent[low : low + 10 * ROWS_BACK] = jnp.zeros((10 * ROWS_BACK, 128), F32)

    def put(value, f):
        for pair in range(2):
            cols = slice(pair * 128, (pair + 1) * 128)
            both = separate(value[: 2 * KEPT_COLS, cols], value[2 * KEPT_COLS :, cols])
            for k in range(2):
                g = 2 * pair + k
                first = both[k][:KEPT_COLS].reshape(11, 8, 128)
                second = both[k][KEPT_COLS:].reshape(11, 8, 128)
                even = jnp.where(upper_kept, first, pltpu.roll(second, 4, 1))
                odd = jnp.where(upper_kept, pltpu.roll(first, 4, 1), second)
                for j in range(11):
                    low = (g * 32 + 2 * j) * ROWS_BACK + f * 8
                    sent[low : low + 8, :] = even[j]
                    sent[low + ROWS_BACK : low + ROWS_BACK + 8, :] = odd[j]

    for k in range(3):
        put(slots(lines[k]), k)
    put(kx_kept * slots(lines[3]) + kz * slots(lines[5]), 3)
    put(slots(lines[4]), 4)
    sent[pl.ds(8 * FIELDS_BACK, 128, stride=ROWS_BACK), :] = jnp.broadcast_to(
        sums[0:1, :], (128, 128)
    )


def update_kernel(cutoffs, damping_of, power_of, came, state, groups, yf_high, yf_low, made_state):
    grp = lax.axis_index("grp")
    slab = lax.axis_index(SLAB)
    index = lax.broadcasted_iota(jnp.int32, (64, N), 0)
    picked = slot_rows(groups[...], index + grp * 64)
    mode_z = jnp.sum(jnp.where(picked, signed_row((64, N)), 0), axis=1, keepdims=True)
    mode_y = signed_row((1, N))
    slot = lax.broadcasted_iota(jnp.int32, (64, 1), 0)
    source_grp = lax.broadcasted_iota(jnp.int32, (128, 128), 0) // 32
    total = came[pl.ds(8 * FIELDS_BACK, 128, stride=ROWS_BACK), :]
    total = jnp.sum(jnp.where(source_grp == grp, total, 0.0), axis=0, keepdims=True)
    quarter = lanes((1, 128)) // 32
    means = [
        jnp.sum(jnp.where(quarter == k, total, 0.0), axis=1, keepdims=True) / (GMODES * KX * N)
        for k in range(4)
    ]
    forcings = [
        (power_of[grp * 2 + k] - means[k]) / (2.0 * (means[2 + k] + EPSILON)) for k in range(2)
    ]
    forcing = jnp.where(slot < GMODES, forcings[0], forcings[1])
    damping = jnp.where(slot < GMODES, damping_of[grp * 2], damping_of[grp * 2 + 1])
    wave_z = mode_z.astype(F32) * WAVE
    wave_y = mode_y.astype(F32) * WAVE
    kept_zy = (96 * jnp.abs(mode_z) <= cutoffs[2] * N) & (96 * jnp.abs(mode_y) <= cutoffs[1] * N)
    table = (yf_high[...], yf_low[...])
    wave_zy = wave_y * wave_y + wave_z * wave_z
    grown = 1.0 + TIME_STEP * forcing
    rotation = TIME_STEP * CORIOLIS
    top = lax.broadcasted_iota(jnp.int32, (128, 128), 0) == 0
    sign = jnp.where(lanes((128, 128)) < 64, 1.0, -1.0).astype(F32)
    for x in range(4):
        mode_x = slab * 4 + x
        wave_x = mode_x.astype(F32) * WAVE
        kept = kept_zy & (96 * mode_x <= cutoffs[0] * N)

        def spectral(f):
            near, far = (
                came[pl.ds(f * 8 + low * 4 + x, 128, stride=ROWS_BACK), :] for low in range(2)
            )
            odd = near - far
            odd = jnp.where(top, odd, sign * pltpu.roll(odd, 64, 1))
            both = jnp.concatenate([(near + far).T, odd.T], axis=1)
            got = product(split(both), table, ((1,), (0,)))
            return got[0:64], got[64:128]

        moments = [spectral(f) for f in range(3)]
        partial_b = spectral(3)
        flux_y = spectral(4)
        source = [partial_b[k] + wave_y * flux_y[k] for k in range(2)]
        sources = (source[1], -source[0])
        wave_sq = wave_x * wave_x + wave_zy
        implicit = 1.0 + TIME_STEP * damping * wave_sq
        square = implicit * implicit
        first = 1.0 / (square + rotation * rotation)
        second = 1.0 / (square + TIME_STEP * TIME_STEP * BRUNT_SQUARED)
        inverse_sq = 1.0 / jnp.where(wave_sq == 0, 1.0, wave_sq)
        for k in range(2):
            flows = [
                jnp.concatenate(
                    [state[f * 2 + k, pl.ds(h * 4 + x, 64, stride=8), :] for h in range(2)], axis=1
                )
                for f in range(4)
            ]
            right = [
                flows[f] * grown + jnp.where(kept, TIME_STEP * moments[f][k], 0.0)
                for f in range(3)
            ]
            right_b = flows[3] + jnp.where(kept, TIME_STEP * sources[k], 0.0)
            new_x = (implicit * right[0] + rotation * right[1]) * first
            new_y = (implicit * right[1] - rotation * right[0]) * first
            new_z = (implicit * right[2] + TIME_STEP * right_b) * second
            new_b = (implicit * right_b - TIME_STEP * BRUNT_SQUARED * right[2]) * second
            inner = (wave_x * new_x + wave_y * new_y + wave_z * new_z) * inverse_sq
            made = (new_x - wave_x * inner, new_y - wave_y * inner, new_z - wave_z * inner, new_b)
            for f in range(4):
                for h in range(2):
                    made_state[f * 2 + k, pl.ds(h * 4 + x, 64, stride=8), :] = made[f][
                        :, h * 128 : (h + 1) * 128
                    ]


VM = pl.BlockSpec(memory_space=pltpu.VMEM)
SM = pl.BlockSpec(memory_space=pltpu.SMEM)


def granted(mebibytes):
    return pltpu.CompilerParams(vmem_limit_bytes=mebibytes << 20)


def shards(state, kz_group, cutoffs, damping, power):
    y_inverse, z_table, x_inverse, x_forward, y_forward = tables()
    groups = kz_group.reshape(1, N)
    rows = state.reshape(4, 2, 64, 4, 2, 128).transpose(0, 1, 2, 4, 3, 5).reshape(8, 512, 128)

    sent, sums = pl.pallas_call(
        send_kernel,
        out_shape=(
            jax.ShapeDtypeStruct((128 * ROWS_OUT, 128), F32),
            jax.ShapeDtypeStruct((8, 128), F32),
        ),
        in_specs=[VM] * 3,
        out_specs=(VM, VM),
        compiler_params=granted(SEND_MIB),
        name="send",
    )(rows, *y_inverse)
    came = lax.all_to_all(sent.reshape(128, ROWS_OUT, 128), ALL, 0, 0, tiled=True)

    back = pl.pallas_call(
        grid_kernel,
        out_shape=jax.ShapeDtypeStruct((128 * ROWS_BACK, 128), F32),
        in_specs=[VM] * 9,
        out_specs=VM,
        scratch_shapes=[
            pltpu.VMEM((N, N), BF16),
            pltpu.VMEM((N, N), BF16),
            pltpu.VMEM((7, 256, 512), F32),
            pltpu.VMEM((7, 256, 512), F32),
            pltpu.VMEM((6, 4 * KEPT_COLS, N), F32),
        ],
        compiler_params=granted(GRID_MIB),
        name="grid",
    )(came, sums, groups, *z_table, *x_inverse, *x_forward)
    came = lax.all_to_all(back.reshape(128, 1, ROWS_BACK * 128), ALL, 0, 0, tiled=True)

    made = pl.pallas_call(
        update_kernel,
        out_shape=jax.ShapeDtypeStruct((8, 512, 128), F32),
        in_specs=[SM] * 3 + [VM] * 5,
        out_specs=VM,
        compiler_params=granted(UPDATE_MIB),
        name="update",
    )(cutoffs, damping, power, came.reshape(128 * ROWS_BACK, 128), rows, groups, *y_forward)
    made = made.reshape(4, 2, 64, 2, 4, 128).transpose(0, 1, 2, 4, 3, 5)
    return made.reshape(4, 2, 64, 4, N)


def solution(mesh):
    finer = Mesh(
        mesh.devices.reshape(mesh.shape["grp"], 4, 4, 2), ("grp", "slab_0", "slab_1", "slab_2")
    )
    return jax.shard_map(
        shards,
        mesh=finer,
        in_specs=(P(None, None, "grp", SLAB, None), P(), P(), P(), P()),
        out_specs=P(None, None, "grp", SLAB, None),
        check_vma=False,
    )
```

time: 144 us -> 111 us (0.77)
  Pallas kernels: 26.6 us -> 13.4 us
  blocking collectives: 99.7 us -> 93.5 us
  local copies, waits for them, and re-layouts: 9.74 us -> 3.58 us
  starting transfers between devices: 4.81 us -> 0 us
  other arithmetic: 1.46 us -> 0 us
    psum x3 -> x0, blocking collectives: 46.8 us -> none  [shards(): sums = lax.psum(sums, axis)]
    all_to_all x0 -> x1, blocking collectives: none -> 40.8 us  [shards(): lax.all_to_all(back.reshape(128, 1, ROWS_BACK * 128), ALL, 0, 0, tiled=True)]
    pallas_call x2, Pallas kernels: 19.8 us -> 10.9 us  [the longest x1 6.18 us: shards(): pl.pallas_call(grid_kernel, out_shape=jax.ShapeDtypeStruct((128 * ROWS_BA...]
    all_to_all x1 -> x0, starting transfers between devices: 4.81 us -> none  [shards(): came = lax.all_to_all(back, ALL, 0, 0, tiled=True)]
    pallas_call x1, Pallas kernels: 6.8 us -> 2.49 us  [shards(): pl.pallas_call(send_kernel, out_shape=(jax.ShapeDtypeStruct((128 * ROWS_O...]
    reshape x1 -> x0, local copies, waits for them, and re-layouts: 4.26 us -> none  [shards(): return made.reshape(4, 4, 2, 64, N).transpose(0, 2, 3, 1, 4)]
    transpose x1 -> x0, local copies, waits for them, and re-layouts: 3.28 us -> none  [shards(): rows = state.transpose(0, 3, 1, 2, 4).reshape(16, 128, N)]
    unnamed x12 -> x32, local copies, waits for them, and re-layouts: 1.53 us -> 3.58 us
  transfers between devices with their start and end apart: 1 -> 0, of which waited for: 0 -> 0; matrix products, arithmetic and copies ran while one was open for 1% -> 0% of each run, Pallas kernels for 0% -> 0%
where the time goes in v1:
time: 111 us
  blocking collectives  93.5 us (84%)
  Pallas kernels  13.4 us (12%)
  local copies, waits for them, and re-layouts  3.58 us (3%)
    all_to_all x1, blocking collectives, shards(): lax.all_to_all(sent.reshape(128, ROWS_OUT, 128), ALL, 0, 0, tiled=True)  52.7 us
    all_to_all x1, blocking collectives, shards(): lax.all_to_all(back.reshape(128, 1, ROWS_BACK * 128), ALL, 0, 0, tiled=True)  40.8 us
    pallas_call x1, Pallas kernels, shards(): pl.pallas_call(grid_kernel, out_shape=jax.ShapeDtypeStruct((128 * ROWS_BA...  6.18 us
    pallas_call x1, Pallas kernels, shards(): pl.pallas_call(update_kernel, out_shape=jax.ShapeDtypeStruct((8, 512, 128...  4.75 us
    unnamed x32, local copies, waits for them, and re-layouts  3.58 us
    pallas_call x1, Pallas kernels, shards(): pl.pallas_call(send_kernel, out_shape=(jax.ShapeDtypeStruct((128 * ROWS_O...  2.49 us

profile of v1, /device:TPU:0, one launch (start us, length us, event | category | flops | bytes accessed | tf_op | source)
XLA Modules:
  0.0 110.6 jit_solution(4821460907021720788)
XLA Ops:
  0.0 1.6 %copy-done = f32[4,2,64,4,256]{4,3,2,1,0:T(4,128)S(1)} copy-done((f32[4,2,64,4,256]{4,3,2,1,0:T(4,128)S(1)}, f32[4,2,64,4,256]{4,3,2,1,0:T(4,128)}, u32[]{:S(2)}) %copy-start) | copy-done | bytes 2097176
  1.6 0.9 copy-done.2
  2.5 0.9 copy-done.3
  3.5 2.5 %send.1 = (f32[6144,128]{1,0:T(8,128)S(1)}, f32[8,128]{1,0:T(8,128)S(1)}) custom-call(f32[8,512,128]{2,1,0:T(8,128)S(1)} %bitcast.16, bf16[512,256]{1,0:T(8,128)(2,1)S(1)} %copy-done.3, bf16[512,256]{1,0:T(8,128)(2,1)S(1)} %copy-done.2), custom_call_target="tpu_custom_call" | custom-call | tf_op jit(solution)/shard_map/send/pallas_call | solution.py:421
  6.0 0.0 copy-start.6
  6.0 0.0 copy-start.7
  6.0 0.0 copy-start.8
  6.0 0.0 copy-start.9
  6.0 0.0 copy-start.10
  6.1 0.0 copy-start.11
  6.1 0.0 copy-start.12
  6.1 52.7 %all_to_all.10.came = f32[128,48,128]{2,1,0:T(8,128)S(1)} all-to-all(f32[128,48,128]{2,1,0:T(8,128)S(1)} %bitcast.18), channel_id=1, replica_groups=mesh['grp'=4,'slab_0'=4,'slab_1'=4,'slab_2'=2] {'grp','slab_0','slab_1',..., dimensions={0} | all-to-all | bytes 6291456 | tf_op jit(solution)/shard_map/all_to_all | solution.py:432
  58.7 0.0 copy-done.6
  58.7 0.0 copy-done.7
  58.7 0.0 copy-done.8
  58.7 0.0 copy-done.9
  58.7 0.0 copy-done.10
  58.8 0.0 copy-done.11
  58.8 0.0 copy-done.12
  58.8 6.2 %grid.1 = f32[5248,128]{1,0:T(8,128)S(1)} custom-call(f32[128,48,128]{2,1,0:T(8,128)S(1)} %all_to_all.10.came, f32[8,128]{1,0:T(8,128)S(1)} %get-tuple-element.8.sums, s32[1,256]{1,0:T(1,128)S(1)} %bitcast.19, bf16[256,256]{1,0:T(8,128)(2,1)S(1)} %copy-done.9, bf16[256,256]{1,0:T(8,128)(2,1)S(1)} %copy-done.8, bf16[256,256]{1,0:T(8,128)(2,1)S(1)} %copy-done.7, ...), custom_call_target="tpu_custom_call" | custom-call | tf_op jit(solution)/shard_map/grid/pallas_call | solution.py:434
  65.0 0.0 copy-start.1
  65.0 0.0 copy-start.4
  65.0 0.0 copy-start.5
  65.0 0.0 copy-start.13
  65.0 0.0 copy-start.14
  65.0 0.0 copy-start.15
  65.0 40.8 %all_to_all.11 = f32[128,1,5248]{2,1,0:T(1,128)S(1)} all-to-all(f32[128,1,5248]{2,1,0:T(1,128)S(1)} %bitcast.14), channel_id=1, replica_groups=mesh['grp'=4,'slab_0'=4,'slab_1'=4,'slab_2'=2] {'grp','slab_0','slab_1',..., dimensions={0} | all-to-all | bytes 5373952 | tf_op jit(solution)/shard_map/all_to_all | solution.py:449
  105.9 0.0 copy-done.1
  105.9 0.0 copy-done.4
  105.9 0.0 copy-done.5
  105.9 0.0 copy-done.13
  105.9 4.8 %update.1 = f32[8,512,128]{2,1,0:T(8,128)} custom-call(s32[3]{0:T(128)S(1)} %copy-done.13, f32[8]{0:T(128)S(1)} %copy-done.14, f32[8]{0:T(128)S(1)} %copy-done.15, f32[5248,128]{1,0:T(8,128)S(1)} %bitcast.15, f32[8,512,128]{2,1,0:T(8,128)S(1)} %bitcast.17, s32[1,256]{1,0:T(1,128)S(1)} %bitcast.20, bf16[256,256]{1,0:T(8,128)(2,1)S(1)} %copy-done.5, ...), custom_call_target="tpu_custom_call" | custom-call | tf_op jit(solution)/shard_map/update/pallas_call | solution.py:451
  (5 shorter events, 0.0 us)
Async XLA Ops:
  0.0 1.6 %copy-start = (f32[4,2,64,4,256]{4,3,2,1,0:T(4,128)S(1)}, f32[4,2,64,4,256]{4,3,2,1,0:T(4,128)}, u32[]{:S(2)}) copy-start(f32[4,2,64,4,256]{4,3,2,1,0:T(4,128)} %param.15) | copy-start | bytes 6291460
  1.6 0.9 copy-start.2
  2.5 0.9 copy-start.3
  6.0 52.7 %copy-start.6 = (bf16[256,256]{1,0:T(8,128)(2,1)S(1)}, bf16[256,256]{1,0:T(8,128)(2,1)}, u32[]{:S(2)}) copy-start(bf16[256,256]{1,0:T(8,128)(2,1)} %constant.25.clone.xi_low) | copy-start | bytes 393220
  6.0 52.7 %copy-start.7 = (bf16[256,256]{1,0:T(8,128)(2,1)S(1)}, bf16[256,256]{1,0:T(8,128)(2,1)}, u32[]{:S(2)}) copy-start(bf16[256,256]{1,0:T(8,128)(2,1)} %constant.24.clone.xi_high) | copy-start | bytes 393220
  6.0 52.7 %copy-start.8 = (bf16[256,256]{1,0:T(8,128)(2,1)S(1)}, bf16[256,256]{1,0:T(8,128)(2,1)}, u32[]{:S(2)}) copy-start(bf16[256,256]{1,0:T(8,128)(2,1)} %constant.23.clone.zt_low) | copy-start | bytes 393220
  6.0 52.7 %copy-start.9 = (bf16[256,256]{1,0:T(8,128)(2,1)S(1)}, bf16[256,256]{1,0:T(8,128)(2,1)}, u32[]{:S(2)}) copy-start(bf16[256,256]{1,0:T(8,128)(2,1)} %constant.22.clone.zt_high) | copy-start | bytes 393220
  6.0 52.7 %copy-start.10 = (bf16[176,256]{1,0:T(8,128)(2,1)S(1)}, bf16[176,256]{1,0:T(8,128)(2,1)}, u32[]{:S(2)}) copy-start(bf16[176,256]{1,0:T(8,128)(2,1)} %constant.27.clone.xf_low) | copy-start | bytes 270340
  6.1 52.7 %copy-start.11 = (bf16[176,256]{1,0:T(8,128)(2,1)S(1)}, bf16[176,256]{1,0:T(8,128)(2,1)}, u32[]{:S(2)}) copy-start(bf16[176,256]{1,0:T(8,128)(2,1)} %constant.26.clone.xf_high) | copy-start | bytes 270340
  6.1 52.7 %copy-start.12 = (s32[256]{0:T(256)S(1)}, s32[256]{0:T(256)}, u32[]{:S(2)}) copy-start(s32[256]{0:T(256)} %param.16) | copy-start | bytes 3076
  65.0 40.9 %copy-start.1 = (f32[4,2,64,4,256]{4,3,2,1,0:T(4,128)S(1)}, f32[4,2,64,4,256]{4,3,2,1,0:T(4,128)}, u32[]{:S(2)}) copy-start(f32[4,2,64,4,256]{4,3,2,1,0:T(4,128)} %param.15) | copy-start | bytes 6291460
  65.0 40.9 %copy-start.4 = (bf16[256,256]{1,0:T(8,128)(2,1)S(1)}, bf16[256,256]{1,0:T(8,128)(2,1)}, u32[]{:S(2)}) copy-start(bf16[256,256]{1,0:T(8,128)(2,1)} %constant.29.clone.yf_low) | copy-start | bytes 393220
  65.0 40.9 %copy-start.5 = (bf16[256,256]{1,0:T(8,128)(2,1)S(1)}, bf16[256,256]{1,0:T(8,128)(2,1)}, u32[]{:S(2)}) copy-start(bf16[256,256]{1,0:T(8,128)(2,1)} %constant.28.clone.yf_high) | copy-start | bytes 393220
  65.0 40.9 %copy-start.13 = (s32[3]{0:T(128)S(1)}, s32[3]{0:T(128)}, u32[]{:S(2)}) copy-start(s32[3]{0:T(128)} %cutoffs.1) | copy-start | bytes 40
  65.0 40.9 %copy-start.14 = (f32[8]{0:T(128)S(1)}, f32[8]{0:T(128)}, u32[]{:S(2)}) copy-start(f32[8]{0:T(128)} %damping_of.1) | copy-start | bytes 100
  65.0 40.9 %copy-start.15 = (f32[8]{0:T(128)S(1)}, f32[8]{0:T(128)}, u32[]{:S(2)}) copy-start(f32[8]{0:T(128)} %power_of.1) | copy-start | bytes 100

commit v2 on v1

--- a/solution.py
+++ b/solution.py
@@ -33,7 +33,7 @@
 
 SEND_MIB = 24
 GRID_MIB = 40
-UPDATE_MIB = 24
+UPDATE_MIB = 28
 
 F32 = jnp.float32
 BF16 = jnp.bfloat16
@@ -108,7 +108,82 @@
     return lax.broadcasted_iota(jnp.int32, shape, len(shape) - 1)
 
 
-def send_kernel(state, w_high, w_low, sent, sums):
+def fill_factors(cutoffs, damping_of, groups, factors):
+    grp = lax.axis_index("grp")
+    slab = lax.axis_index(SLAB)
+    here = slot_rows(groups[...], lax.broadcasted_iota(jnp.int32, (64, N), 0) + grp * 64)
+    mode_z = jnp.sum(jnp.where(here, signed_row((64, N)), 0), axis=1, keepdims=True)
+    mode_y = signed_row((1, N))
+    slot = lax.broadcasted_iota(jnp.int32, (64, 1), 0)
+    damping = jnp.where(slot < GMODES, damping_of[grp * 2], damping_of[grp * 2 + 1])
+    wave_z = mode_z.astype(F32) * WAVE
+    wave_y = mode_y.astype(F32) * WAVE
+    kept_zy = (96 * jnp.abs(mode_z) <= cutoffs[2] * N) & (96 * jnp.abs(mode_y) <= cutoffs[1] * N)
+    wave_zy = wave_y * wave_y + wave_z * wave_z
+    rotation = TIME_STEP * CORIOLIS
+    for x in range(4):
+        mode_x = slab * 4 + x
+        wave_x = mode_x.astype(F32) * WAVE
+        kept = kept_zy & (96 * mode_x <= cutoffs[0] * N)
+        wave_sq = wave_x * wave_x + wave_zy
+        implicit = 1.0 + TIME_STEP * damping * wave_sq
+        square = implicit * implicit
+        first = 1.0 / (square + rotation * rotation)
+        second = 1.0 / (square + TIME_STEP * TIME_STEP * BRUNT_SQUARED)
+        factors[0, x] = implicit * first
+        factors[1, x] = rotation * first
+        factors[2, x] = implicit * second
+        factors[3, x] = TIME_STEP * second
+        factors[4, x] = 1.0 / jnp.where(wave_sq == 0, 1.0, wave_sq)
+        factors[5, x] = jnp.where(kept, TIME_STEP, 0.0)
+    factors[6, 0] = jnp.broadcast_to(wave_z, (64, N))
+
+
+def send_kernel(
+    cutoffs_far,
+    damping_far,
+    groups_far,
+    state_far,
+    w_high_far,
+    w_low_far,
+    sent,
+    sums,
+    factors,
+    cutoffs,
+    damping_of,
+    groups,
+    state,
+    w_high,
+    w_low,
+    sems,
+):
+    copies = {}
+
+    def fetch(key, source, target, k):
+        copies[key] = pltpu.make_async_copy(source, target, sems.at[k])
+        copies[key].start()
+
+    small = ((groups_far, groups), (cutoffs_far, cutoffs), (damping_far, damping_of))
+    for k, (source, target) in enumerate(small):
+        fetch(k, source, target, 8 + k)
+    order = (1, 0, 2, 3)
+    for k, low in enumerate((0, N)):
+        rows = pl.ds(low, N)
+        if k == 0:
+            fetch("high0", w_high_far.at[rows], w_high.at[rows], 0)
+            fetch("state1", state_far.at[pl.ds(2, 2)], state.at[pl.ds(2, 2)], 1)
+            fetch("low0", w_low_far.at[rows], w_low.at[rows], 2)
+        else:
+            fetch("high1", w_high_far.at[rows], w_high.at[rows], 3)
+            fetch("low1", w_low_far.at[rows], w_low.at[rows], 4)
+    for k, f in enumerate(order[1:]):
+        rows = pl.ds(2 * f, 2)
+        fetch("state" + str(f), state_far.at[rows], state.at[rows], 5 + k)
+
+    for k in range(3):
+        copies[k].wait()
+    fill_factors(cutoffs, damping_of, groups, factors)
+
     sign = jnp.where(lanes((HALF, 128)) < 64, -1.0, 1.0).astype(F32)
     top = lax.broadcasted_iota(jnp.int32, (HALF, 128), 0) == 0
     flux = jnp.zeros((128, N), F32)
@@ -118,36 +193,36 @@
         for low, value in ((0, even + odd), (1, even - odd)):
             sent[pl.ds(slot * 8 + low * 4 + x, 128, stride=ROWS_OUT), :] = value
 
-    for pair in range(2):
-        pieces = []
-        for f in range(4):
-            rows = []
-            for x in (2 * pair, 2 * pair + 1):
-                for part in range(2):
-                    rows.append(
-                        jnp.concatenate(
-                            [
-                                state[f * 2 + part, pl.ds(h * 4 + x, 64, stride=8), :]
-                                for h in range(2)
-                            ],
-                            axis=1,
-                        )
+    def piece(f, pair):
+        rows = []
+        for x in (2 * pair, 2 * pair + 1):
+            for part in range(2):
+                rows.append(
+                    jnp.concatenate(
+                        [state[f * 2 + part, pl.ds(h * 4 + x, 64, stride=8), :] for h in range(2)],
+                        axis=1,
                     )
-            pieces.append(jnp.concatenate(rows, axis=0))
-        flow_x, flow_y, flow_z, buoyant = pieces
-        moved = flow_z * buoyant
-        held = 0.5 * (
-            flow_x * flow_x
-            + flow_y * flow_y
-            + flow_z * flow_z
-            + buoyant * buoyant * (1.0 / BRUNT_SQUARED)
-        )
-        flux = flux + (moved[:128] + moved[128:])
-        energy = energy + (held[:128] + held[128:])
-        for f in range(4):
-            derived = {0: 4, 2: 5}.get(f)
-            count = 512 if derived else 256
-            made = product((w_high[:count], w_low[:count]), split(pieces[f]), ((1,), (1,)))
+                )
+        return jnp.concatenate(rows, axis=0)
+
+    for f in order:
+        if f == 1:
+            for key in ("high0", "low0", "high1", "low1", "state1", "state0"):
+                copies[key].wait()
+        if f == 2:
+            copies["state2"].wait()
+            copies["state3"].wait()
+        derived = {0: 4, 2: 5}.get(f)
+        count = 512 if derived else 256
+        share = 0.5 / BRUNT_SQUARED if f == 3 else 0.5
+        for pair in range(2):
+            value = piece(f, pair)
+            square = share * (value * value)
+            energy = energy + (square[:128] + square[128:])
+            if f == 3:
+                moved = value * piece(2, pair)
+                flux = flux + (moved[:128] + moved[128:])
+            made = product((w_high[:count], w_low[:count]), split(value), ((1,), (1,)))
             for k in range(2):
                 x = pair * 2 + k
                 cols = slice(k * 128, (k + 1) * 128)
@@ -324,14 +399,14 @@
     )
 
 
-def update_kernel(cutoffs, damping_of, power_of, came, state, groups, yf_high, yf_low, made_state):
+BLOCK = 8
+
+
+def update_kernel(
+    power_of, came, state, factors, yf_high, yf_low, made_far, left_high, left_low, got, made_state, sems
+):
     grp = lax.axis_index("grp")
     slab = lax.axis_index(SLAB)
-    index = lax.broadcasted_iota(jnp.int32, (64, N), 0)
-    picked = slot_rows(groups[...], index + grp * 64)
-    mode_z = jnp.sum(jnp.where(picked, signed_row((64, N)), 0), axis=1, keepdims=True)
-    mode_y = signed_row((1, N))
-    slot = lax.broadcasted_iota(jnp.int32, (64, 1), 0)
     source_grp = lax.broadcasted_iota(jnp.int32, (128, 128), 0) // 32
     total = came[pl.ds(8 * FIELDS_BACK, 128, stride=ROWS_BACK), :]
     total = jnp.sum(jnp.where(source_grp == grp, total, 0.0), axis=0, keepdims=True)
@@ -340,73 +415,91 @@
         jnp.sum(jnp.where(quarter == k, total, 0.0), axis=1, keepdims=True) / (GMODES * KX * N)
         for k in range(4)
     ]
-    forcings = [
-        (power_of[grp * 2 + k] - means[k]) / (2.0 * (means[2 + k] + EPSILON)) for k in range(2)
+    grown = [
+        1.0
+        + TIME_STEP * ((power_of[grp * 2 + k] - means[k]) / (2.0 * (means[2 + k] + EPSILON)))
+        for k in range(2)
     ]
-    forcing = jnp.where(slot < GMODES, forcings[0], forcings[1])
-    damping = jnp.where(slot < GMODES, damping_of[grp * 2], damping_of[grp * 2 + 1])
-    wave_z = mode_z.astype(F32) * WAVE
-    wave_y = mode_y.astype(F32) * WAVE
-    kept_zy = (96 * jnp.abs(mode_z) <= cutoffs[2] * N) & (96 * jnp.abs(mode_y) <= cutoffs[1] * N)
-    table = (yf_high[...], yf_low[...])
-    wave_zy = wave_y * wave_y + wave_z * wave_z
-    grown = 1.0 + TIME_STEP * forcing
-    rotation = TIME_STEP * CORIOLIS
-    top = lax.broadcasted_iota(jnp.int32, (128, 128), 0) == 0
-    sign = jnp.where(lanes((128, 128)) < 64, 1.0, -1.0).astype(F32)
+    wave_y = signed_row((1, N)).astype(F32) * WAVE
+    start = lanes((64, 128)) == 0
     for x in range(4):
-        mode_x = slab * 4 + x
-        wave_x = mode_x.astype(F32) * WAVE
-        kept = kept_zy & (96 * mode_x <= cutoffs[0] * N)
-
-        def spectral(f):
+        for f in range(FIELDS_BACK):
             near, far = (
                 came[pl.ds(f * 8 + low * 4 + x, 128, stride=ROWS_BACK), :] for low in range(2)
             )
-            odd = near - far
-            odd = jnp.where(top, odd, sign * pltpu.roll(odd, 64, 1))
-            both = jnp.concatenate([(near + far).T, odd.T], axis=1)
-            got = product(split(both), table, ((1,), (0,)))
-            return got[0:64], got[64:128]
-
-        moments = [spectral(f) for f in range(3)]
-        partial_b = spectral(3)
-        flux_y = spectral(4)
-        source = [partial_b[k] + wave_y * flux_y[k] for k in range(2)]
-        sources = (source[1], -source[0])
-        wave_sq = wave_x * wave_x + wave_zy
-        implicit = 1.0 + TIME_STEP * damping * wave_sq
-        square = implicit * implicit
-        first = 1.0 / (square + rotation * rotation)
-        second = 1.0 / (square + TIME_STEP * TIME_STEP * BRUNT_SQUARED)
-        inverse_sq = 1.0 / jnp.where(wave_sq == 0, 1.0, wave_sq)
-        for k in range(2):
-            flows = [
-                jnp.concatenate(
-                    [state[f * 2 + k, pl.ds(h * 4 + x, 64, stride=8), :] for h in range(2)], axis=1
+            even, odd = (near + far).T, (near - far).T
+            real, imag = odd[:64], odd[64:]
+            turned = (jnp.where(start, real, imag), jnp.where(start, imag, -real))
+            rows = slice((x * FIELDS_BACK + f) * 128, (x * FIELDS_BACK + f + 1) * 128)
+            left_high[rows, :128], left_low[rows, :128] = split(even)
+            left_high[rows, 128:], left_low[rows, 128:] = split(jnp.concatenate(turned, axis=0))
+        rows = slice(x * FIELDS_BACK * 128, (x + 1) * FIELDS_BACK * 128)
+        got[rows] = product(
+            (left_high[rows], left_low[rows]), (yf_high[...], yf_low[...]), ((1,), (0,))
+        )
+
+    copies = []
+    for block in range(64 // BLOCK):
+        low = block * BLOCK
+        grow = grown[low // GMODES]
+        wave_z = factors[6, 0, low : low + BLOCK]
+        for x in range(4):
+            wave_x = (slab * 4 + x).astype(F32) * WAVE
+            main, turn, slow, lift, inverse_sq, step = (
+                factors[k, x, low : low + BLOCK] for k in range(6)
+            )
+
+            def part(f, k):
+                row = (x * FIELDS_BACK + f) * 128 + k * 64 + low
+                return got[row : row + BLOCK]
+
+            for k in range(2):
+                source = part(3, 1 - k) + wave_y * part(4, 1 - k)
+                flows = [
+                    jnp.concatenate(
+                        [
+                            state[f * 2 + k, pl.ds(low * 8 + h * 4 + x, BLOCK, stride=8), :]
+                            for h in range(2)
+                        ],
+                        axis=1,
+                    )
+                    for f in range(4)
+                ]
+                right = [flows[f] * grow + step * part(f, k) for f in range(3)]
+                right_b = flows[3] + (step * source if k == 0 else -(step * source))
+                new_x = main * right[0] + turn * right[1]
+                new_y = main * right[1] - turn * right[0]
+                new_z = slow * right[2] + lift * right_b
+                new_b = slow * right_b - BRUNT_SQUARED * (lift * right[2])
+                inner = (wave_x * new_x + wave_y * new_y + wave_z * new_z) * inverse_sq
+                made = (
+                    new_x - wave_x * inner,
+                    new_y - wave_y * inner,
+                    new_z - wave_z * inner,
+                    new_b,
                 )
-                for f in range(4)
-            ]
-            right = [
-                flows[f] * grown + jnp.where(kept, TIME_STEP * moments[f][k], 0.0)
-                for f in range(3)
-            ]
-            right_b = flows[3] + jnp.where(kept, TIME_STEP * sources[k], 0.0)
-            new_x = (implicit * right[0] + rotation * right[1]) * first
-            new_y = (implicit * right[1] - rotation * right[0]) * first
-            new_z = (implicit * right[2] + TIME_STEP * right_b) * second
-            new_b = (implicit * right_b - TIME_STEP * BRUNT_SQUARED * right[2]) * second
-            inner = (wave_x * new_x + wave_y * new_y + wave_z * new_z) * inverse_sq
-            made = (new_x - wave_x * inner, new_y - wave_y * inner, new_z - wave_z * inner, new_b)
-            for f in range(4):
-                for h in range(2):
-                    made_state[f * 2 + k, pl.ds(h * 4 + x, 64, stride=8), :] = made[f][
-                        :, h * 128 : (h + 1) * 128
-                    ]
+                for f in range(4):
+                    for h in range(2):
+                        rows = pl.ds(low * 8 + h * 4 + x, BLOCK, stride=8)
+                        made_state[f * 2 + k, rows, :] = made[f][:, h * 128 : (h + 1) * 128]
+        if block % 2:
+            rows = pl.ds((block - 1) * BLOCK * 8, 2 * BLOCK * 8)
+            copy = pltpu.make_async_copy(
+                made_state.at[:, rows], made_far.at[:, rows], sems.at[block // 2]
+            )
+            copy.start()
+            copies.append(copy)
+    for copy in copies:
+        copy.wait()
 
 
 VM = pl.BlockSpec(memory_space=pltpu.VMEM)
 SM = pl.BlockSpec(memory_space=pltpu.SMEM)
+HBM = pl.BlockSpec(memory_space=pltpu.HBM)
+
+
+def far(array):
+    return pltpu.with_memory_space_constraint(array, pltpu.HBM)
 
 
 def granted(mebibytes):
@@ -418,17 +511,27 @@
     groups = kz_group.reshape(1, N)
     rows = state.reshape(4, 2, 64, 4, 2, 128).transpose(0, 1, 2, 4, 3, 5).reshape(8, 512, 128)
 
-    sent, sums = pl.pallas_call(
+    sent, sums, factors = pl.pallas_call(
         send_kernel,
         out_shape=(
             jax.ShapeDtypeStruct((128 * ROWS_OUT, 128), F32),
             jax.ShapeDtypeStruct((8, 128), F32),
+            jax.ShapeDtypeStruct((7, 4, 64, N), F32),
         ),
-        in_specs=[VM] * 3,
-        out_specs=(VM, VM),
+        in_specs=[HBM] * 6,
+        out_specs=(VM, VM, VM),
+        scratch_shapes=[
+            pltpu.SMEM((3,), jnp.int32),
+            pltpu.SMEM((GROUPS,), F32),
+            pltpu.VMEM((1, N), jnp.int32),
+            pltpu.VMEM((8, 512, 128), F32),
+            pltpu.VMEM((512, N), BF16),
+            pltpu.VMEM((512, N), BF16),
+            pltpu.SemaphoreType.DMA((11,)),
+        ],
         compiler_params=granted(SEND_MIB),
         name="send",
-    )(rows, *y_inverse)
+    )(*(far(a) for a in (cutoffs, damping, groups, rows, *y_inverse)))
     came = lax.all_to_all(sent.reshape(128, ROWS_OUT, 128), ALL, 0, 0, tiled=True)
 
     back = pl.pallas_call(
@@ -451,11 +554,18 @@
     made = pl.pallas_call(
         update_kernel,
         out_shape=jax.ShapeDtypeStruct((8, 512, 128), F32),
-        in_specs=[SM] * 3 + [VM] * 5,
-        out_specs=VM,
+        in_specs=[SM] + [VM] * 5,
+        out_specs=HBM,
+        scratch_shapes=[
+            pltpu.VMEM((20 * 128, N), BF16),
+            pltpu.VMEM((20 * 128, N), BF16),
+            pltpu.VMEM((20 * 128, N), F32),
+            pltpu.VMEM((8, 512, 128), F32),
+            pltpu.SemaphoreType.DMA((32 // BLOCK,)),
+        ],
         compiler_params=granted(UPDATE_MIB),
         name="update",
-    )(cutoffs, damping, power, came.reshape(128 * ROWS_BACK, 128), rows, groups, *y_forward)
+    )(power, came.reshape(128 * ROWS_BACK, 128), rows, factors, *y_forward)
     made = made.reshape(4, 2, 64, 2, 4, 128).transpose(0, 1, 2, 4, 3, 5)
     return made.reshape(4, 2, 64, 4, N)
 

time: 111 us -> 109 us (0.982)
  local copies, waits for them, and re-layouts: 3.58 us -> 0.07 us
  Pallas kernels: 13.4 us -> 14.9 us
    unnamed x32 -> x22, local copies, waits for them, and re-layouts: 3.58 us -> 0.07 us
    pallas_call x1, Pallas kernels: 2.49 us -> 4.23 us  [shards(): pl.pallas_call(send_kernel, out_shape=(jax.ShapeDtypeStruct((128 * ROWS_O...]
where the time goes in v2:
time: 109 us
  blocking collectives  93.5 us (86%)
  Pallas kernels  14.9 us (14%)
    all_to_all x1, blocking collectives, shards(): lax.all_to_all(sent.reshape(128, ROWS_OUT, 128), ALL, 0, 0, tiled=True)  52.6 us
    all_to_all x1, blocking collectives, shards(): lax.all_to_all(back.reshape(128, 1, ROWS_BACK * 128), ALL, 0, 0, tiled=True)  40.8 us
    pallas_call x1, Pallas kernels, shards(): pl.pallas_call(grid_kernel, out_shape=jax.ShapeDtypeStruct((128 * ROWS_BA...  6.17 us
    pallas_call x1, Pallas kernels, shards(): pl.pallas_call(update_kernel, out_shape=jax.ShapeDtypeStruct((8, 512, 128...  4.47 us
    pallas_call x1, Pallas kernels, shards(): pl.pallas_call(send_kernel, out_shape=(jax.ShapeDtypeStruct((128 * ROWS_O...  4.23 us

profile of v2, /device:TPU:0, one launch (start us, length us, event | category | flops | bytes accessed | tf_op | source)
XLA Modules:
  0.0 108.7 jit_solution(4929951968086863950)
XLA Ops:
  0.0 4.2 %send.1 = (f32[6144,128]{1,0:T(8,128)S(1)}, f32[8,128]{1,0:T(8,128)S(1)}, f32[7,4,64,256]{3,2,1,0:T(8,128)S(1)}) custom-call(s32[3]{0:T(128)} %cutoffs_far.1, f32[8]{0:T(128)} %damping_far.1, s32[1,256]{1,0:T(1,128)} %bitcast.19, f32[8,512,128]{2,1,0:T(8,128)} %bitcast.16, bf16[512,256]{1,0:T(8,128)(2,1)} %constant.20.clone.w_high_far, ...), custom_call_target="tpu_custom_call" | custom-call | tf_op jit(solution)/shard_map/send/pallas_call | solution.py:514
  4.2 0.0 copy-start.3
  4.2 0.0 copy-start.4
  4.3 0.0 copy-start.5
  4.3 0.0 copy-start.6
  4.3 0.0 copy-start.7
  4.3 0.0 copy-start.8
  4.3 0.0 copy-start.9
  4.3 52.6 %all_to_all.10.came = f32[128,48,128]{2,1,0:T(8,128)S(1)} all-to-all(f32[128,48,128]{2,1,0:T(8,128)S(1)} %bitcast.18), channel_id=1, replica_groups=mesh['grp'=4,'slab_0'=4,'slab_1'=4,'slab_2'=2] {'grp','slab_0','slab_1',..., dimensions={0} | all-to-all | bytes 6291456 | tf_op jit(solution)/shard_map/all_to_all | solution.py:535
  57.0 0.0 copy-done.3
  57.0 0.0 copy-done.4
  57.0 0.0 copy-done.5
  57.0 0.0 copy-done.6
  57.0 0.0 copy-done.7
  57.0 0.0 copy-done.8
  57.0 0.0 copy-done.9
  57.0 6.2 %grid.1 = f32[5248,128]{1,0:T(8,128)S(1)} custom-call(f32[128,48,128]{2,1,0:T(8,128)S(1)} %all_to_all.10.came, f32[8,128]{1,0:T(8,128)S(1)} %get-tuple-element.9.sums, s32[1,256]{1,0:T(1,128)S(1)} %bitcast.20, bf16[256,256]{1,0:T(8,128)(2,1)S(1)} %copy-done.6, bf16[256,256]{1,0:T(8,128)(2,1)S(1)} %copy-done.5, bf16[256,256]{1,0:T(8,128)(2,1)S(1)} %copy-done.4, ...), custom_call_target="tpu_custom_call" | custom-call | tf_op jit(solution)/shard_map/grid/pallas_call | solution.py:537
  63.2 0.0 copy-start
  63.2 0.0 copy-start.1
  63.2 0.0 copy-start.2
  63.2 0.0 copy-start.10
  63.2 40.8 %all_to_all.11 = f32[128,1,5248]{2,1,0:T(1,128)S(1)} all-to-all(f32[128,1,5248]{2,1,0:T(1,128)S(1)} %bitcast.14), channel_id=1, replica_groups=mesh['grp'=4,'slab_0'=4,'slab_1'=4,'slab_2'=2] {'grp','slab_0','slab_1',..., dimensions={0} | all-to-all | bytes 5373952 | tf_op jit(solution)/shard_map/all_to_all | solution.py:552
  104.1 0.0 copy-done
  104.1 0.0 copy-done.1
  104.1 0.0 copy-done.2
  104.1 0.0 copy-done.10
  104.1 4.5 %update.1 = f32[8,512,128]{2,1,0:T(8,128)} custom-call(f32[8]{0:T(128)S(1)} %copy-done.10, f32[5248,128]{1,0:T(8,128)S(1)} %bitcast.15, f32[8,512,128]{2,1,0:T(8,128)S(1)} %bitcast.17, f32[7,4,64,256]{3,2,1,0:T(8,128)S(1)} %get-tuple-element.10.factors, bf16[256,256]{1,0:T(8,128)(2,1)S(1)} %copy-done.2, bf16[256,256]{1,0:T(8,128)(2,1)S(1)} %copy-done.1), custom_call_target="tpu_custom_call" | custom-call | tf_op jit(solution)/shard_map/update/pallas_call | solution.py:554
Async XLA Ops:
  4.2 52.7 %copy-start.3 = (bf16[256,256]{1,0:T(8,128)(2,1)S(1)}, bf16[256,256]{1,0:T(8,128)(2,1)}, u32[]{:S(2)}) copy-start(bf16[256,256]{1,0:T(8,128)(2,1)} %constant.25.clone.xi_low) | copy-start | bytes 393220
  4.2 52.7 %copy-start.4 = (bf16[256,256]{1,0:T(8,128)(2,1)S(1)}, bf16[256,256]{1,0:T(8,128)(2,1)}, u32[]{:S(2)}) copy-start(bf16[256,256]{1,0:T(8,128)(2,1)} %constant.24.clone.xi_high) | copy-start | bytes 393220
  4.3 52.7 %copy-start.5 = (bf16[256,256]{1,0:T(8,128)(2,1)S(1)}, bf16[256,256]{1,0:T(8,128)(2,1)}, u32[]{:S(2)}) copy-start(bf16[256,256]{1,0:T(8,128)(2,1)} %constant.23.clone.zt_low) | copy-start | bytes 393220
  4.3 52.7 %copy-start.6 = (bf16[256,256]{1,0:T(8,128)(2,1)S(1)}, bf16[256,256]{1,0:T(8,128)(2,1)}, u32[]{:S(2)}) copy-start(bf16[256,256]{1,0:T(8,128)(2,1)} %constant.22.clone.zt_high) | copy-start | bytes 393220
  4.3 52.7 %copy-start.7 = (bf16[176,256]{1,0:T(8,128)(2,1)S(1)}, bf16[176,256]{1,0:T(8,128)(2,1)}, u32[]{:S(2)}) copy-start(bf16[176,256]{1,0:T(8,128)(2,1)} %constant.27.clone.xf_low) | copy-start | bytes 270340
  4.3 52.7 %copy-start.8 = (bf16[176,256]{1,0:T(8,128)(2,1)S(1)}, bf16[176,256]{1,0:T(8,128)(2,1)}, u32[]{:S(2)}) copy-start(bf16[176,256]{1,0:T(8,128)(2,1)} %constant.26.clone.xf_high) | copy-start | bytes 270340
  4.3 52.7 %copy-start.9 = (s32[256]{0:T(256)S(1)}, s32[256]{0:T(256)}, u32[]{:S(2)}) copy-start(s32[256]{0:T(256)} %param.16) | copy-start | bytes 3076
  63.2 40.9 %copy-start = (f32[4,2,64,4,256]{4,3,2,1,0:T(4,128)S(1)}, f32[4,2,64,4,256]{4,3,2,1,0:T(4,128)}, u32[]{:S(2)}) copy-start(f32[4,2,64,4,256]{4,3,2,1,0:T(4,128)} %param.15) | copy-start | bytes 6291460
  63.2 40.9 %copy-start.1 = (bf16[256,256]{1,0:T(8,128)(2,1)S(1)}, bf16[256,256]{1,0:T(8,128)(2,1)}, u32[]{:S(2)}) copy-start(bf16[256,256]{1,0:T(8,128)(2,1)} %constant.29.clone.yf_low) | copy-start | bytes 393220
  63.2 40.9 %copy-start.2 = (bf16[256,256]{1,0:T(8,128)(2,1)S(1)}, bf16[256,256]{1,0:T(8,128)(2,1)}, u32[]{:S(2)}) copy-start(bf16[256,256]{1,0:T(8,128)(2,1)} %constant.28.clone.yf_high) | copy-start | bytes 393220
  63.2 40.8 %copy-start.10 = (f32[8]{0:T(128)S(1)}, f32[8]{0:T(128)}, u32[]{:S(2)}) copy-start(f32[8]{0:T(128)} %power_of.1) | copy-start | bytes 100

commit v3 on v2

--- a/solution.py
+++ b/solution.py
@@ -108,7 +108,7 @@
     return lax.broadcasted_iota(jnp.int32, shape, len(shape) - 1)
 
 
-def fill_factors(cutoffs, damping_of, groups, factors):
+def fill_factors(cutoffs, damping_of, power_of, groups, factors):
     grp = lax.axis_index("grp")
     slab = lax.axis_index(SLAB)
     here = slot_rows(groups[...], lax.broadcasted_iota(jnp.int32, (64, N), 0) + grp * 64)
@@ -137,11 +137,14 @@
         factors[4, x] = 1.0 / jnp.where(wave_sq == 0, 1.0, wave_sq)
         factors[5, x] = jnp.where(kept, TIME_STEP, 0.0)
     factors[6, 0] = jnp.broadcast_to(wave_z, (64, N))
+    power = jnp.where(slot < GMODES, power_of[grp * 2], power_of[grp * 2 + 1])
+    factors[6, 1] = jnp.broadcast_to(power, (64, N))
 
 
 def send_kernel(
     cutoffs_far,
     damping_far,
+    power_far,
     groups_far,
     state_far,
     w_high_far,
@@ -151,6 +154,7 @@
     factors,
     cutoffs,
     damping_of,
+    power_of,
     groups,
     state,
     w_high,
@@ -163,7 +167,12 @@
         copies[key] = pltpu.make_async_copy(source, target, sems.at[k])
         copies[key].start()
 
-    small = ((groups_far, groups), (cutoffs_far, cutoffs), (damping_far, damping_of))
+    small = (
+        (groups_far, groups),
+        (cutoffs_far, cutoffs),
+        (damping_far, damping_of),
+        (power_far, power_of),
+    )
     for k, (source, target) in enumerate(small):
         fetch(k, source, target, 8 + k)
     order = (1, 0, 2, 3)
@@ -180,9 +189,9 @@
         rows = pl.ds(2 * f, 2)
         fetch("state" + str(f), state_far.at[rows], state.at[rows], 5 + k)
 
-    for k in range(3):
+    for k in range(4):
         copies[k].wait()
-    fill_factors(cutoffs, damping_of, groups, factors)
+    fill_factors(cutoffs, damping_of, power_of, groups, factors)
 
     sign = jnp.where(lanes((HALF, 128)) < 64, -1.0, 1.0).astype(F32)
     top = lax.broadcasted_iota(jnp.int32, (HALF, 128), 0) == 0
@@ -403,7 +412,7 @@
 
 
 def update_kernel(
-    power_of, came, state, factors, yf_high, yf_low, made_far, left_high, left_low, got, made_state, sems
+    came, state, factors, yf_high, yf_low, made_far, left_high, left_low, got, made_state, sems
 ):
     grp = lax.axis_index("grp")
     slab = lax.axis_index(SLAB)
@@ -414,11 +423,6 @@
     means = [
         jnp.sum(jnp.where(quarter == k, total, 0.0), axis=1, keepdims=True) / (GMODES * KX * N)
         for k in range(4)
-    ]
-    grown = [
-        1.0
-        + TIME_STEP * ((power_of[grp * 2 + k] - means[k]) / (2.0 * (means[2 + k] + EPSILON)))
-        for k in range(2)
     ]
     wave_y = signed_row((1, N)).astype(F32) * WAVE
     start = lanes((64, 128)) == 0
@@ -438,20 +442,30 @@
             (left_high[rows], left_low[rows]), (yf_high[...], yf_low[...]), ((1,), (0,))
         )
 
-    copies = []
-    for block in range(64 // BLOCK):
-        low = block * BLOCK
-        grow = grown[low // GMODES]
-        wave_z = factors[6, 0, low : low + BLOCK]
+    blocks = 64 // BLOCK
+
+    def out_copy(block):
+        rows = pl.ds(pl.multiple_of(block * (8 * BLOCK), 8 * BLOCK), 8 * BLOCK)
+        return pltpu.make_async_copy(
+            made_state.at[:, rows], made_far.at[:, rows], sems.at[block]
+        )
+
+    def step_block(block, carry):
+        low = pl.multiple_of(block * BLOCK, BLOCK)
+        high = block * BLOCK >= GMODES
+        flux = jnp.where(high, means[1], means[0])
+        energy = jnp.where(high, means[3], means[2])
+        wave_z = factors[6, 0, pl.ds(low, BLOCK)]
+        power = factors[6, 1, pl.ds(low, BLOCK)]
+        grow = 1.0 + TIME_STEP * ((power - flux) / (2.0 * (energy + EPSILON)))
         for x in range(4):
             wave_x = (slab * 4 + x).astype(F32) * WAVE
             main, turn, slow, lift, inverse_sq, step = (
-                factors[k, x, low : low + BLOCK] for k in range(6)
+                factors[k, x, pl.ds(low, BLOCK)] for k in range(6)
             )
 
             def part(f, k):
-                row = (x * FIELDS_BACK + f) * 128 + k * 64 + low
-                return got[row : row + BLOCK]
+                return got[pl.ds((x * FIELDS_BACK + f) * 128 + k * 64 + low, BLOCK)]
 
             for k in range(2):
                 source = part(3, 1 - k) + wave_y * part(4, 1 - k)
@@ -482,19 +496,15 @@
                     for h in range(2):
                         rows = pl.ds(low * 8 + h * 4 + x, BLOCK, stride=8)
                         made_state[f * 2 + k, rows, :] = made[f][:, h * 128 : (h + 1) * 128]
-        if block % 2:
-            rows = pl.ds((block - 1) * BLOCK * 8, 2 * BLOCK * 8)
-            copy = pltpu.make_async_copy(
-                made_state.at[:, rows], made_far.at[:, rows], sems.at[block // 2]
-            )
-            copy.start()
-            copies.append(copy)
-    for copy in copies:
-        copy.wait()
+        out_copy(block).start()
+        return carry
+
+    lax.fori_loop(0, blocks, step_block, 0)
+    for block in range(blocks):
+        out_copy(block).wait()
 
 
 VM = pl.BlockSpec(memory_space=pltpu.VMEM)
-SM = pl.BlockSpec(memory_space=pltpu.SMEM)
 HBM = pl.BlockSpec(memory_space=pltpu.HBM)
 
 
@@ -518,20 +528,21 @@
             jax.ShapeDtypeStruct((8, 128), F32),
             jax.ShapeDtypeStruct((7, 4, 64, N), F32),
         ),
-        in_specs=[HBM] * 6,
+        in_specs=[HBM] * 7,
         out_specs=(VM, VM, VM),
         scratch_shapes=[
             pltpu.SMEM((3,), jnp.int32),
+            pltpu.SMEM((GROUPS,), F32),
             pltpu.SMEM((GROUPS,), F32),
             pltpu.VMEM((1, N), jnp.int32),
             pltpu.VMEM((8, 512, 128), F32),
             pltpu.VMEM((512, N), BF16),
             pltpu.VMEM((512, N), BF16),
-            pltpu.SemaphoreType.DMA((11,)),
+            pltpu.SemaphoreType.DMA((12,)),
         ],
         compiler_params=granted(SEND_MIB),
         name="send",
-    )(*(far(a) for a in (cutoffs, damping, groups, rows, *y_inverse)))
+    )(*(far(a) for a in (cutoffs, damping, power, groups, rows, *y_inverse)))
     came = lax.all_to_all(sent.reshape(128, ROWS_OUT, 128), ALL, 0, 0, tiled=True)
 
     back = pl.pallas_call(
@@ -554,18 +565,18 @@
     made = pl.pallas_call(
         update_kernel,
         out_shape=jax.ShapeDtypeStruct((8, 512, 128), F32),
-        in_specs=[SM] + [VM] * 5,
+        in_specs=[VM] * 5,
         out_specs=HBM,
         scratch_shapes=[
             pltpu.VMEM((20 * 128, N), BF16),
             pltpu.VMEM((20 * 128, N), BF16),
             pltpu.VMEM((20 * 128, N), F32),
             pltpu.VMEM((8, 512, 128), F32),
-            pltpu.SemaphoreType.DMA((32 // BLOCK,)),
+            pltpu.SemaphoreType.DMA((64 // BLOCK,)),
         ],
         compiler_params=granted(UPDATE_MIB),
         name="update",
-    )(power, came.reshape(128 * ROWS_BACK, 128), rows, factors, *y_forward)
+    )(came.reshape(128 * ROWS_BACK, 128), rows, factors, *y_forward)
     made = made.reshape(4, 2, 64, 2, 4, 128).transpose(0, 1, 2, 4, 3, 5)
     return made.reshape(4, 2, 64, 4, N)
 

time: 109 us -> 108 us (level)
  Pallas kernels: 14.9 us -> 13.7 us
    pallas_call x1, Pallas kernels: 4.47 us -> 3.27 us  [shards(): pl.pallas_call(update_kernel, out_shape=jax.ShapeDtypeStruct((8, 512, 128...]
where the time goes in v3:
time: 108 us; the launch traced here: 107 us
  blocking collectives  93.5 us (87%)
  Pallas kernels  13.7 us (13%)
    all_to_all x1, blocking collectives, shards(): lax.all_to_all(sent.reshape(128, ROWS_OUT, 128), ALL, 0, 0, tiled=True)  52.6 us
    all_to_all x1, blocking collectives, shards(): lax.all_to_all(back.reshape(128, 1, ROWS_BACK * 128), ALL, 0, 0, tiled=True)  40.8 us
    pallas_call x1, Pallas kernels, shards(): pl.pallas_call(grid_kernel, out_shape=jax.ShapeDtypeStruct((128 * ROWS_BA...  6.17 us
    pallas_call x1, Pallas kernels, shards(): pl.pallas_call(send_kernel, out_shape=(jax.ShapeDtypeStruct((128 * ROWS_O...  4.23 us
    pallas_call x1, Pallas kernels, shards(): pl.pallas_call(update_kernel, out_shape=jax.ShapeDtypeStruct((8, 512, 128...  3.27 us

profile of v3, /device:TPU:0, one launch (start us, length us, event | category | flops | bytes accessed | tf_op | source)
XLA Modules:
  0.0 107.3 jit_solution(1976675320570096420)
XLA Ops:
  0.0 4.2 %send.1 = (f32[6144,128]{1,0:T(8,128)S(1)}, f32[8,128]{1,0:T(8,128)S(1)}, f32[7,4,64,256]{3,2,1,0:T(8,128)S(1)}) custom-call(s32[3]{0:T(128)} %cutoffs_far.1, f32[8]{0:T(128)} %damping_far.1, f32[8]{0:T(128)} %power_far.1, s32[1,256]{1,0:T(1,128)} %bitcast.19, f32[8,512,128]{2,1,0:T(8,128)} %bitcast.16, bf16[512,256]{1,0:T(8,128)(2,1)} %constant.20.clone.w_high_far, ...), custom_call_target="tpu_custom_call" | custom-call | tf_op jit(solution)/shard_map/send/pallas_call | solution.py:524
  4.2 0.0 copy-start.3
  4.3 0.0 copy-start.4
  4.3 0.0 copy-start.5
  4.3 0.0 copy-start.6
  4.3 0.0 copy-start.7
  4.3 0.0 copy-start.8
  4.3 0.0 copy-start.9
  4.3 52.6 %all_to_all.10.came = f32[128,48,128]{2,1,0:T(8,128)S(1)} all-to-all(f32[128,48,128]{2,1,0:T(8,128)S(1)} %bitcast.18), channel_id=1, replica_groups=mesh['grp'=4,'slab_0'=4,'slab_1'=4,'slab_2'=2] {'grp','slab_0','slab_1',..., dimensions={0} | all-to-all | bytes 6291456 | tf_op jit(solution)/shard_map/all_to_all | solution.py:546
  57.0 0.0 copy-done.3
  57.0 0.0 copy-done.4
  57.0 0.0 copy-done.5
  57.0 0.0 copy-done.6
  57.0 0.0 copy-done.7
  57.0 0.0 copy-done.8
  57.0 0.0 copy-done.9
  57.0 6.2 %grid.1 = f32[5248,128]{1,0:T(8,128)S(1)} custom-call(f32[128,48,128]{2,1,0:T(8,128)S(1)} %all_to_all.10.came, f32[8,128]{1,0:T(8,128)S(1)} %get-tuple-element.9.sums, s32[1,256]{1,0:T(1,128)S(1)} %bitcast.20, bf16[256,256]{1,0:T(8,128)(2,1)S(1)} %copy-done.6, bf16[256,256]{1,0:T(8,128)(2,1)S(1)} %copy-done.5, bf16[256,256]{1,0:T(8,128)(2,1)S(1)} %copy-done.4, ...), custom_call_target="tpu_custom_call" | custom-call | tf_op jit(solution)/shard_map/grid/pallas_call | solution.py:548
  63.2 0.0 copy-start
  63.2 0.0 copy-start.1
  63.2 0.0 copy-start.2
  63.2 40.8 %all_to_all.11 = f32[128,1,5248]{2,1,0:T(1,128)S(1)} all-to-all(f32[128,1,5248]{2,1,0:T(1,128)S(1)} %bitcast.14), channel_id=1, replica_groups=mesh['grp'=4,'slab_0'=4,'slab_1'=4,'slab_2'=2] {'grp','slab_0','slab_1',..., dimensions={0} | all-to-all | bytes 5373952 | tf_op jit(solution)/shard_map/all_to_all | solution.py:563
  104.1 0.0 copy-done
  104.1 0.0 copy-done.1
  104.1 0.0 copy-done.2
  104.1 3.3 %update.1 = f32[8,512,128]{2,1,0:T(8,128)} custom-call(f32[5248,128]{1,0:T(8,128)S(1)} %bitcast.15, f32[8,512,128]{2,1,0:T(8,128)S(1)} %bitcast.17, f32[7,4,64,256]{3,2,1,0:T(8,128)S(1)} %get-tuple-element.10.factors, bf16[256,256]{1,0:T(8,128)(2,1)S(1)} %copy-done.2, bf16[256,256]{1,0:T(8,128)(2,1)S(1)} %copy-done.1), custom_call_target="tpu_custom_call" | custom-call | tf_op jit(solution)/shard_map/update/pallas_call | solution.py:565
Async XLA Ops:
  4.2 52.7 %copy-start.3 = (bf16[256,256]{1,0:T(8,128)(2,1)S(1)}, bf16[256,256]{1,0:T(8,128)(2,1)}, u32[]{:S(2)}) copy-start(bf16[256,256]{1,0:T(8,128)(2,1)} %constant.25.clone.xi_low) | copy-start | bytes 393220
  4.3 52.7 %copy-start.4 = (bf16[256,256]{1,0:T(8,128)(2,1)S(1)}, bf16[256,256]{1,0:T(8,128)(2,1)}, u32[]{:S(2)}) copy-start(bf16[256,256]{1,0:T(8,128)(2,1)} %constant.24.clone.xi_high) | copy-start | bytes 393220
  4.3 52.7 %copy-start.5 = (bf16[256,256]{1,0:T(8,128)(2,1)S(1)}, bf16[256,256]{1,0:T(8,128)(2,1)}, u32[]{:S(2)}) copy-start(bf16[256,256]{1,0:T(8,128)(2,1)} %constant.23.clone.zt_low) | copy-start | bytes 393220
  4.3 52.7 %copy-start.6 = (bf16[256,256]{1,0:T(8,128)(2,1)S(1)}, bf16[256,256]{1,0:T(8,128)(2,1)}, u32[]{:S(2)}) copy-start(bf16[256,256]{1,0:T(8,128)(2,1)} %constant.22.clone.zt_high) | copy-start | bytes 393220
  4.3 52.7 %copy-start.7 = (bf16[176,256]{1,0:T(8,128)(2,1)S(1)}, bf16[176,256]{1,0:T(8,128)(2,1)}, u32[]{:S(2)}) copy-start(bf16[176,256]{1,0:T(8,128)(2,1)} %constant.27.clone.xf_low) | copy-start | bytes 270340
  4.3 52.7 %copy-start.8 = (bf16[176,256]{1,0:T(8,128)(2,1)S(1)}, bf16[176,256]{1,0:T(8,128)(2,1)}, u32[]{:S(2)}) copy-start(bf16[176,256]{1,0:T(8,128)(2,1)} %constant.26.clone.xf_high) | copy-start | bytes 270340
  4.3 52.7 %copy-start.9 = (s32[256]{0:T(256)S(1)}, s32[256]{0:T(256)}, u32[]{:S(2)}) copy-start(s32[256]{0:T(256)} %param.16) | copy-start | bytes 3076
  63.2 40.9 %copy-start = (f32[4,2,64,4,256]{4,3,2,1,0:T(4,128)S(1)}, f32[4,2,64,4,256]{4,3,2,1,0:T(4,128)}, u32[]{:S(2)}) copy-start(f32[4,2,64,4,256]{4,3,2,1,0:T(4,128)} %param.15) | copy-start | bytes 6291460
  63.2 40.8 %copy-start.1 = (bf16[256,256]{1,0:T(8,128)(2,1)S(1)}, bf16[256,256]{1,0:T(8,128)(2,1)}, u32[]{:S(2)}) copy-start(bf16[256,256]{1,0:T(8,128)(2,1)} %constant.29.clone.yf_low) | copy-start | bytes 393220
  63.2 40.8 %copy-start.2 = (bf16[256,256]{1,0:T(8,128)(2,1)S(1)}, bf16[256,256]{1,0:T(8,128)(2,1)}, u32[]{:S(2)}) copy-start(bf16[256,256]{1,0:T(8,128)(2,1)} %constant.28.clone.yf_high) | copy-start | bytes 393220

commit v4 on v3

--- a/solution.py
+++ b/solution.py
@@ -28,8 +28,8 @@
 SCALE = 1.0 / 4096.0
 FIELDS_OUT = 6
 FIELDS_BACK = 5
-ROWS_OUT = 8 * FIELDS_OUT
-ROWS_BACK = 8 * FIELDS_BACK + 1
+ROWS_OUT = 8 * FIELDS_OUT + 1
+ROWS_BACK = 8 * FIELDS_BACK
 
 SEND_MIB = 24
 GRID_MIB = 40
@@ -150,7 +150,6 @@
     w_high_far,
     w_low_far,
     sent,
-    sums,
     factors,
     cutoffs,
     damping_of,
@@ -252,12 +251,11 @@
             part = part + pltpu.roll(part, 64, 1)
             part = part + pltpu.roll(part, 32, 1)
             total = jnp.where(quarter == 2 * k + which, part, total)
-    sums[...] = jnp.broadcast_to(total, (8, 128))
+    sent[pl.ds(8 * FIELDS_OUT, 128, stride=ROWS_OUT), :] = jnp.broadcast_to(total, (128, 128))
 
 
 def grid_kernel(
     came,
-    sums,
     groups,
     zt_high,
     zt_low,
@@ -266,6 +264,7 @@
     xf_high,
     xf_low,
     sent,
+    totals,
     wz_high,
     wz_low,
     rows_z,
@@ -297,8 +296,9 @@
     def field(f):
         pieces = []
         for g in range(4):
-            tiles = came[g * 32 : (g + 1) * 32, f * 8 : (f + 1) * 8, :].reshape(16, 2, 8, 128)
-            even, odd = tiles[:, 0], tiles[:, 1]
+            lows = [(g * 32 + k) * ROWS_OUT + f * 8 for k in range(32)]
+            even = jnp.stack([came[low : low + 8, :] for low in lows[0::2]])
+            odd = jnp.stack([came[low : low + 8, :] for low in lows[1::2]])
             first = jnp.where(upper, even, pltpu.roll(odd, 4, 1))
             second = jnp.where(upper, pltpu.roll(even, 4, 1), odd)
             pieces.append(
@@ -403,22 +403,20 @@
         put(slots(lines[k]), k)
     put(kx_kept * slots(lines[3]) + kz * slots(lines[5]), 3)
     put(slots(lines[4]), 4)
-    sent[pl.ds(8 * FIELDS_BACK, 128, stride=ROWS_BACK), :] = jnp.broadcast_to(
-        sums[0:1, :], (128, 128)
-    )
+    source_grp = lax.broadcasted_iota(jnp.int32, (128, 128), 0) // 32
+    total = came[pl.ds(8 * FIELDS_OUT, 128, stride=ROWS_OUT), :]
+    total = jnp.where(source_grp == lax.axis_index("grp"), total, 0.0)
+    totals[...] = jnp.broadcast_to(jnp.sum(total, axis=0, keepdims=True), (8, 128))
 
 
 BLOCK = 8
 
 
 def update_kernel(
-    came, state, factors, yf_high, yf_low, made_far, left_high, left_low, got, made_state, sems
+    came, totals, state, factors, yf_high, yf_low, made_far, left_high, left_low, got, made_state, sems
 ):
-    grp = lax.axis_index("grp")
     slab = lax.axis_index(SLAB)
-    source_grp = lax.broadcasted_iota(jnp.int32, (128, 128), 0) // 32
-    total = came[pl.ds(8 * FIELDS_BACK, 128, stride=ROWS_BACK), :]
-    total = jnp.sum(jnp.where(source_grp == grp, total, 0.0), axis=0, keepdims=True)
+    total = totals[0:1, :]
     quarter = lanes((1, 128)) // 32
     means = [
         jnp.sum(jnp.where(quarter == k, total, 0.0), axis=1, keepdims=True) / (GMODES * KX * N)
@@ -521,15 +519,14 @@
     groups = kz_group.reshape(1, N)
     rows = state.reshape(4, 2, 64, 4, 2, 128).transpose(0, 1, 2, 4, 3, 5).reshape(8, 512, 128)
 
-    sent, sums, factors = pl.pallas_call(
+    sent, factors = pl.pallas_call(
         send_kernel,
         out_shape=(
             jax.ShapeDtypeStruct((128 * ROWS_OUT, 128), F32),
-            jax.ShapeDtypeStruct((8, 128), F32),
             jax.ShapeDtypeStruct((7, 4, 64, N), F32),
         ),
         in_specs=[HBM] * 7,
-        out_specs=(VM, VM, VM),
+        out_specs=(VM, VM),
         scratch_shapes=[
             pltpu.SMEM((3,), jnp.int32),
             pltpu.SMEM((GROUPS,), F32),
@@ -543,13 +540,16 @@
         compiler_params=granted(SEND_MIB),
         name="send",
     )(*(far(a) for a in (cutoffs, damping, power, groups, rows, *y_inverse)))
-    came = lax.all_to_all(sent.reshape(128, ROWS_OUT, 128), ALL, 0, 0, tiled=True)
-
-    back = pl.pallas_call(
+    came = lax.all_to_all(sent.reshape(128, 1, ROWS_OUT * 128), ALL, 0, 0, tiled=True)
+
+    back, totals = pl.pallas_call(
         grid_kernel,
-        out_shape=jax.ShapeDtypeStruct((128 * ROWS_BACK, 128), F32),
-        in_specs=[VM] * 9,
-        out_specs=VM,
+        out_shape=(
+            jax.ShapeDtypeStruct((128 * ROWS_BACK, 128), F32),
+            jax.ShapeDtypeStruct((8, 128), F32),
+        ),
+        in_specs=[VM] * 8,
+        out_specs=(VM, VM),
         scratch_shapes=[
             pltpu.VMEM((N, N), BF16),
             pltpu.VMEM((N, N), BF16),
@@ -559,13 +559,13 @@
         ],
         compiler_params=granted(GRID_MIB),
         name="grid",
-    )(came, sums, groups, *z_table, *x_inverse, *x_forward)
-    came = lax.all_to_all(back.reshape(128, 1, ROWS_BACK * 128), ALL, 0, 0, tiled=True)
+    )(came.reshape(128 * ROWS_OUT, 128), groups, *z_table, *x_inverse, *x_forward)
+    came = lax.all_to_all(back.reshape(128, ROWS_BACK, 128), ALL, 0, 0, tiled=True)
 
     made = pl.pallas_call(
         update_kernel,
         out_shape=jax.ShapeDtypeStruct((8, 512, 128), F32),
-        in_specs=[VM] * 5,
+        in_specs=[VM] * 6,
         out_specs=HBM,
         scratch_shapes=[
             pltpu.VMEM((20 * 128, N), BF16),
@@ -576,7 +576,7 @@
         ],
         compiler_params=granted(UPDATE_MIB),
         name="update",
-    )(came.reshape(128 * ROWS_BACK, 128), rows, factors, *y_forward)
+    )(came.reshape(128 * ROWS_BACK, 128), totals, rows, factors, *y_forward)
     made = made.reshape(4, 2, 64, 2, 4, 128).transpose(0, 1, 2, 4, 3, 5)
     return made.reshape(4, 2, 64, 4, N)
 

time: 108 us -> 107 us (level)
  no operation moved by 1% of the time
where the time goes in v4:
time: 107 us
  blocking collectives  93.5 us (87%)
  Pallas kernels  13.3 us (12%)
    all_to_all x1, blocking collectives, shards(): lax.all_to_all(sent.reshape(128, 1, ROWS_OUT * 128), ALL, 0, 0, tiled=True)  53.4 us
    all_to_all x1, blocking collectives, shards(): lax.all_to_all(back.reshape(128, ROWS_BACK, 128), ALL, 0, 0, tiled=True)  40.1 us
    pallas_call x1, Pallas kernels, shards(): pl.pallas_call(grid_kernel, out_shape=(jax.ShapeDtypeStruct((128 * ROWS_B...  6.16 us
    pallas_call x1, Pallas kernels, shards(): pl.pallas_call(send_kernel, out_shape=(jax.ShapeDtypeStruct((128 * ROWS_O...  3.72 us
    pallas_call x1, Pallas kernels, shards(): pl.pallas_call(update_kernel, out_shape=jax.ShapeDtypeStruct((8, 512, 128...  3.4 us

profile of v4, /device:TPU:0, one launch (start us, length us, event | category | flops | bytes accessed | tf_op | source)
XLA Modules:
  0.0 107.0 jit_solution(2637293634771103465)
XLA Ops:
  0.0 3.7 %send.1 = (f32[6272,128]{1,0:T(8,128)S(1)}, f32[7,4,64,256]{3,2,1,0:T(8,128)S(1)}) custom-call(s32[3]{0:T(128)} %cutoffs_far.1, f32[8]{0:T(128)} %damping_far.1, f32[8]{0:T(128)} %power_far.1, s32[1,256]{1,0:T(1,128)} %bitcast.21, f32[8,512,128]{2,1,0:T(8,128)} %bitcast.17, bf16[512,256]{1,0:T(8,128)(2,1)} %constant.20.clone.w_high_far, ...), custom_call_target="tpu_custom_call" | custom-call | tf_op jit(solution)/shard_map/send/pallas_call | solution.py:522
  3.7 0.0 copy-start.3
  3.7 0.0 copy-start.4
  3.8 0.0 copy-start.5
  3.8 0.0 copy-start.6
  3.8 0.0 copy-start.7
  3.8 0.0 copy-start.8
  3.8 0.0 copy-start.9
  3.8 53.4 %all_to_all.10 = f32[128,1,6272]{2,1,0:T(1,128)S(1)} all-to-all(f32[128,1,6272]{2,1,0:T(1,128)S(1)} %bitcast.19), channel_id=1, replica_groups=mesh['grp'=4,'slab_0'=4,'slab_1'=4,'slab_2'=2] {'grp','slab_0','slab_1',..., dimensions={0} | all-to-all | bytes 6422528 | tf_op jit(solution)/shard_map/all_to_all | solution.py:543
  57.2 0.0 copy-done.3
  57.2 0.0 copy-done.4
  57.2 0.0 copy-done.5
  57.2 0.0 copy-done.6
  57.2 0.0 copy-done.7
  57.2 0.0 copy-done.8
  57.2 0.0 copy-done.9
  57.2 6.2 %grid.1 = (f32[5120,128]{1,0:T(8,128)S(1)}, f32[8,128]{1,0:T(8,128)S(1)}) custom-call(f32[6272,128]{1,0:T(8,128)S(1)} %bitcast.15, s32[1,256]{1,0:T(1,128)S(1)} %bitcast.22, bf16[256,256]{1,0:T(8,128)(2,1)S(1)} %copy-done.6, bf16[256,256]{1,0:T(8,128)(2,1)S(1)} %copy-done.5, bf16[256,256]{1,0:T(8,128)(2,1)S(1)} %copy-done.4, bf16[256,256]{1,0:T(8,128)(2,1)S(1)} %copy-done.3, ...), custom_call_target="tpu_custom_call" | custom-call | tf_op jit(solution)/shard_map/grid/pallas_call | solution.py:545
  63.4 0.0 copy-start
  63.4 0.0 copy-start.1
  63.4 0.0 copy-start.2
  63.4 40.1 %all_to_all.11 = f32[128,40,128]{2,1,0:T(8,128)S(1)} all-to-all(f32[128,40,128]{2,1,0:T(8,128)S(1)} %bitcast.20), channel_id=1, replica_groups=mesh['grp'=4,'slab_0'=4,'slab_1'=4,'slab_2'=2] {'grp','slab_0','slab_1',..., dimensions={0} | all-to-all | bytes 5242880 | tf_op jit(solution)/shard_map/all_to_all | solution.py:563
  103.5 0.0 copy-done
  103.5 0.0 copy-done.1
  103.5 0.0 copy-done.2
  103.6 3.4 %update.1 = f32[8,512,128]{2,1,0:T(8,128)} custom-call(f32[5120,128]{1,0:T(8,128)S(1)} %bitcast.16, f32[8,128]{1,0:T(8,128)S(1)} %get-tuple-element.11.totals, f32[8,512,128]{2,1,0:T(8,128)S(1)} %bitcast.18, f32[7,4,64,256]{3,2,1,0:T(8,128)S(1)} %get-tuple-element.12.factors, bf16[256,256]{1,0:T(8,128)(2,1)S(1)} %copy-done.2, bf16[256,256]{1,0:T(8,128)(2,1)S(1)} %copy-done.1), custom_call_target="tpu_custom_call" | custom-call | tf_op jit(solution)/shard_map/update/pallas_call | solution.py:565
Async XLA Ops:
  3.7 53.4 %copy-start.3 = (bf16[256,256]{1,0:T(8,128)(2,1)S(1)}, bf16[256,256]{1,0:T(8,128)(2,1)}, u32[]{:S(2)}) copy-start(bf16[256,256]{1,0:T(8,128)(2,1)} %constant.25.clone.xi_low) | copy-start | bytes 393220
  3.7 53.4 %copy-start.4 = (bf16[256,256]{1,0:T(8,128)(2,1)S(1)}, bf16[256,256]{1,0:T(8,128)(2,1)}, u32[]{:S(2)}) copy-start(bf16[256,256]{1,0:T(8,128)(2,1)} %constant.24.clone.xi_high) | copy-start | bytes 393220
  3.8 53.4 %copy-start.5 = (bf16[256,256]{1,0:T(8,128)(2,1)S(1)}, bf16[256,256]{1,0:T(8,128)(2,1)}, u32[]{:S(2)}) copy-start(bf16[256,256]{1,0:T(8,128)(2,1)} %constant.23.clone.zt_low) | copy-start | bytes 393220
  3.8 53.4 %copy-start.6 = (bf16[256,256]{1,0:T(8,128)(2,1)S(1)}, bf16[256,256]{1,0:T(8,128)(2,1)}, u32[]{:S(2)}) copy-start(bf16[256,256]{1,0:T(8,128)(2,1)} %constant.22.clone.zt_high) | copy-start | bytes 393220
  3.8 53.4 %copy-start.7 = (bf16[176,256]{1,0:T(8,128)(2,1)S(1)}, bf16[176,256]{1,0:T(8,128)(2,1)}, u32[]{:S(2)}) copy-start(bf16[176,256]{1,0:T(8,128)(2,1)} %constant.27.clone.xf_low) | copy-start | bytes 270340
  3.8 53.4 %copy-start.8 = (bf16[176,256]{1,0:T(8,128)(2,1)S(1)}, bf16[176,256]{1,0:T(8,128)(2,1)}, u32[]{:S(2)}) copy-start(bf16[176,256]{1,0:T(8,128)(2,1)} %constant.26.clone.xf_high) | copy-start | bytes 270340
  3.8 53.4 %copy-start.9 = (s32[256]{0:T(256)S(1)}, s32[256]{0:T(256)}, u32[]{:S(2)}) copy-start(s32[256]{0:T(256)} %param.16) | copy-start | bytes 3076
  63.4 40.2 %copy-start = (f32[4,2,64,4,256]{4,3,2,1,0:T(4,128)S(1)}, f32[4,2,64,4,256]{4,3,2,1,0:T(4,128)}, u32[]{:S(2)}) copy-start(f32[4,2,64,4,256]{4,3,2,1,0:T(4,128)} %param.15) | copy-start | bytes 6291460
  63.4 40.2 %copy-start.1 = (bf16[256,256]{1,0:T(8,128)(2,1)S(1)}, bf16[256,256]{1,0:T(8,128)(2,1)}, u32[]{:S(2)}) copy-start(bf16[256,256]{1,0:T(8,128)(2,1)} %constant.29.clone.yf_low) | copy-start | bytes 393220
  63.4 40.1 %copy-start.2 = (bf16[256,256]{1,0:T(8,128)(2,1)S(1)}, bf16[256,256]{1,0:T(8,128)(2,1)}, u32[]{:S(2)}) copy-start(bf16[256,256]{1,0:T(8,128)(2,1)} %constant.28.clone.yf_high) | copy-start | bytes 393220

commit v5 on v3

--- a/solution.py
+++ b/solution.py
@@ -30,6 +30,7 @@
 FIELDS_BACK = 5
 ROWS_OUT = 8 * FIELDS_OUT
 ROWS_BACK = 8 * FIELDS_BACK + 1
+ROWS_SPREAD = ROWS_OUT + 1
 
 SEND_MIB = 24
 GRID_MIB = 40
@@ -159,6 +160,7 @@
     state,
     w_high,
     w_low,
+    spread,
     sems,
 ):
     copies = {}
@@ -200,7 +202,7 @@
 
     def put(slot, x, even, odd):
         for low, value in ((0, even + odd), (1, even - odd)):
-            sent[pl.ds(slot * 8 + low * 4 + x, 128, stride=ROWS_OUT), :] = value
+            spread[pl.ds(slot * 8 + low * 4 + x, 128, stride=ROWS_SPREAD), :] = value
 
     def piece(f, pair):
         rows = []
@@ -241,6 +243,10 @@
                     even, odd = made[256:384, cols], made[384:512, cols]
                     even = sign * pltpu.roll(even, 64, 1)
                     put(derived, x, even, jnp.where(top, sign * pltpu.roll(odd, 64, 1), -odd))
+        for slot in (f, derived) if derived else (f,):
+            for device in range(128):
+                low, far_low = device * ROWS_OUT + slot * 8, device * ROWS_SPREAD + slot * 8
+                sent[low : low + 8, :] = spread[far_low : far_low + 8, :]
 
     quarter = lanes((1, 128)) // 32
     total = jnp.zeros((1, 128), F32)
@@ -538,6 +544,7 @@
             pltpu.VMEM((8, 512, 128), F32),
             pltpu.VMEM((512, N), BF16),
             pltpu.VMEM((512, N), BF16),
+            pltpu.VMEM((128 * ROWS_SPREAD, 128), F32),
             pltpu.SemaphoreType.DMA((12,)),
         ],
         compiler_params=granted(SEND_MIB),

time: 108 us -> 107 us (level)
  no operation moved by 1% of the time
where the time goes in v5:
time: 107 us
  blocking collectives  93.5 us (87%)
  Pallas kernels  13.4 us (13%)
    all_to_all x1, blocking collectives, shards(): lax.all_to_all(sent.reshape(128, ROWS_OUT, 128), ALL, 0, 0, tiled=True)  52.7 us
    all_to_all x1, blocking collectives, shards(): lax.all_to_all(back.reshape(128, 1, ROWS_BACK * 128), ALL, 0, 0, tiled=True)  40.8 us
    pallas_call x1, Pallas kernels, shards(): pl.pallas_call(grid_kernel, out_shape=jax.ShapeDtypeStruct((128 * ROWS_BA...  6.17 us
    pallas_call x1, Pallas kernels, shards(): pl.pallas_call(send_kernel, out_shape=(jax.ShapeDtypeStruct((128 * ROWS_O...  3.91 us
    pallas_call x1, Pallas kernels, shards(): pl.pallas_call(update_kernel, out_shape=jax.ShapeDtypeStruct((8, 512, 128...  3.27 us

profile of v5, /device:TPU:0, one launch (start us, length us, event | category | flops | bytes accessed | tf_op | source)
XLA Modules:
  0.0 107.0 jit_solution(13103140780910211180)
XLA Ops:
  0.0 3.9 %send.1 = (f32[6144,128]{1,0:T(8,128)S(1)}, f32[8,128]{1,0:T(8,128)S(1)}, f32[7,4,64,256]{3,2,1,0:T(8,128)S(1)}) custom-call(s32[3]{0:T(128)} %cutoffs_far.1, f32[8]{0:T(128)} %damping_far.1, f32[8]{0:T(128)} %power_far.1, s32[1,256]{1,0:T(1,128)} %bitcast.19, f32[8,512,128]{2,1,0:T(8,128)} %bitcast.16, bf16[512,256]{1,0:T(8,128)(2,1)} %constant.20.clone.w_high_far, ...), custom_call_target="tpu_custom_call" | custom-call | tf_op jit(solution)/shard_map/send/pallas_call | solution.py:530
  3.9 0.0 copy-start.3
  3.9 0.0 copy-start.4
  3.9 0.0 copy-start.5
  4.0 0.0 copy-start.6
  4.0 0.0 copy-start.7
  4.0 0.0 copy-start.8
  4.0 0.0 copy-start.9
  4.0 52.7 %all_to_all.10.came = f32[128,48,128]{2,1,0:T(8,128)S(1)} all-to-all(f32[128,48,128]{2,1,0:T(8,128)S(1)} %bitcast.18), channel_id=1, replica_groups=mesh['grp'=4,'slab_0'=4,'slab_1'=4,'slab_2'=2] {'grp','slab_0','slab_1',..., dimensions={0} | all-to-all | bytes 6291456 | tf_op jit(solution)/shard_map/all_to_all | solution.py:553
  56.7 0.0 copy-done.3
  56.7 0.0 copy-done.4
  56.7 0.0 copy-done.5
  56.7 0.0 copy-done.6
  56.7 0.0 copy-done.7
  56.7 0.0 copy-done.8
  56.7 0.0 copy-done.9
  56.7 6.2 %grid.1 = f32[5248,128]{1,0:T(8,128)S(1)} custom-call(f32[128,48,128]{2,1,0:T(8,128)S(1)} %all_to_all.10.came, f32[8,128]{1,0:T(8,128)S(1)} %get-tuple-element.9.sums, s32[1,256]{1,0:T(1,128)S(1)} %bitcast.20, bf16[256,256]{1,0:T(8,128)(2,1)S(1)} %copy-done.6, bf16[256,256]{1,0:T(8,128)(2,1)S(1)} %copy-done.5, bf16[256,256]{1,0:T(8,128)(2,1)S(1)} %copy-done.4, ...), custom_call_target="tpu_custom_call" | custom-call | tf_op jit(solution)/shard_map/grid/pallas_call | solution.py:555
  62.9 0.0 copy-start
  62.9 0.0 copy-start.1
  62.9 0.0 copy-start.2
  62.9 40.8 %all_to_all.11 = f32[128,1,5248]{2,1,0:T(1,128)S(1)} all-to-all(f32[128,1,5248]{2,1,0:T(1,128)S(1)} %bitcast.14), channel_id=1, replica_groups=mesh['grp'=4,'slab_0'=4,'slab_1'=4,'slab_2'=2] {'grp','slab_0','slab_1',..., dimensions={0} | all-to-all | bytes 5373952 | tf_op jit(solution)/shard_map/all_to_all | solution.py:570
  103.7 0.0 copy-done
  103.7 0.0 copy-done.1
  103.7 0.0 copy-done.2
  103.8 3.3 %update.1 = f32[8,512,128]{2,1,0:T(8,128)} custom-call(f32[5248,128]{1,0:T(8,128)S(1)} %bitcast.15, f32[8,512,128]{2,1,0:T(8,128)S(1)} %bitcast.17, f32[7,4,64,256]{3,2,1,0:T(8,128)S(1)} %get-tuple-element.10.factors, bf16[256,256]{1,0:T(8,128)(2,1)S(1)} %copy-done.2, bf16[256,256]{1,0:T(8,128)(2,1)S(1)} %copy-done.1), custom_call_target="tpu_custom_call" | custom-call | tf_op jit(solution)/shard_map/update/pallas_call | solution.py:572
Async XLA Ops:
  3.9 52.7 %copy-start.3 = (bf16[256,256]{1,0:T(8,128)(2,1)S(1)}, bf16[256,256]{1,0:T(8,128)(2,1)}, u32[]{:S(2)}) copy-start(bf16[256,256]{1,0:T(8,128)(2,1)} %constant.25.clone.xi_low) | copy-start | bytes 393220
  3.9 52.7 %copy-start.4 = (bf16[256,256]{1,0:T(8,128)(2,1)S(1)}, bf16[256,256]{1,0:T(8,128)(2,1)}, u32[]{:S(2)}) copy-start(bf16[256,256]{1,0:T(8,128)(2,1)} %constant.24.clone.xi_high) | copy-start | bytes 393220
  3.9 52.7 %copy-start.5 = (bf16[256,256]{1,0:T(8,128)(2,1)S(1)}, bf16[256,256]{1,0:T(8,128)(2,1)}, u32[]{:S(2)}) copy-start(bf16[256,256]{1,0:T(8,128)(2,1)} %constant.23.clone.zt_low) | copy-start | bytes 393220
  4.0 52.7 %copy-start.6 = (bf16[256,256]{1,0:T(8,128)(2,1)S(1)}, bf16[256,256]{1,0:T(8,128)(2,1)}, u32[]{:S(2)}) copy-start(bf16[256,256]{1,0:T(8,128)(2,1)} %constant.22.clone.zt_high) | copy-start | bytes 393220
  4.0 52.7 %copy-start.7 = (bf16[176,256]{1,0:T(8,128)(2,1)S(1)}, bf16[176,256]{1,0:T(8,128)(2,1)}, u32[]{:S(2)}) copy-start(bf16[176,256]{1,0:T(8,128)(2,1)} %constant.27.clone.xf_low) | copy-start | bytes 270340
  4.0 52.7 %copy-start.8 = (bf16[176,256]{1,0:T(8,128)(2,1)S(1)}, bf16[176,256]{1,0:T(8,128)(2,1)}, u32[]{:S(2)}) copy-start(bf16[176,256]{1,0:T(8,128)(2,1)} %constant.26.clone.xf_high) | copy-start | bytes 270340
  4.0 52.7 %copy-start.9 = (s32[256]{0:T(256)S(1)}, s32[256]{0:T(256)}, u32[]{:S(2)}) copy-start(s32[256]{0:T(256)} %param.16) | copy-start | bytes 3076
  62.9 40.9 %copy-start = (f32[4,2,64,4,256]{4,3,2,1,0:T(4,128)S(1)}, f32[4,2,64,4,256]{4,3,2,1,0:T(4,128)}, u32[]{:S(2)}) copy-start(f32[4,2,64,4,256]{4,3,2,1,0:T(4,128)} %param.15) | copy-start | bytes 6291460
  62.9 40.8 %copy-start.1 = (bf16[256,256]{1,0:T(8,128)(2,1)S(1)}, bf16[256,256]{1,0:T(8,128)(2,1)}, u32[]{:S(2)}) copy-start(bf16[256,256]{1,0:T(8,128)(2,1)} %constant.29.clone.yf_low) | copy-start | bytes 393220
  62.9 40.8 %copy-start.2 = (bf16[256,256]{1,0:T(8,128)(2,1)S(1)}, bf16[256,256]{1,0:T(8,128)(2,1)}, u32[]{:S(2)}) copy-start(bf16[256,256]{1,0:T(8,128)(2,1)} %constant.28.clone.yf_high) | copy-start | bytes 393220

commit v6 on v5

--- a/solution.py
+++ b/solution.py
@@ -218,11 +218,11 @@
 
     for f in order:
         if f == 1:
-            for key in ("high0", "low0", "high1", "low1", "state1", "state0"):
+            for key in ("high0", "low0", "state1"):
                 copies[key].wait()
-        if f == 2:
-            copies["state2"].wait()
-            copies["state3"].wait()
+        if f == 0:
+            for key in ("high1", "low1", "state0", "state2", "state3"):
+                copies[key].wait()
         derived = {0: 4, 2: 5}.get(f)
         count = 512 if derived else 256
         share = 0.5 / BRUNT_SQUARED if f == 3 else 0.5

time: 107 us -> 107 us (level)
  no operation moved by 1% of the time
where the time goes in v6:
time: 107 us
  blocking collectives  93.5 us (87%)
  Pallas kernels  13.2 us (12%)
    all_to_all x1, blocking collectives, shards(): lax.all_to_all(sent.reshape(128, ROWS_OUT, 128), ALL, 0, 0, tiled=True)  52.7 us
    all_to_all x1, blocking collectives, shards(): lax.all_to_all(back.reshape(128, 1, ROWS_BACK * 128), ALL, 0, 0, tiled=True)  40.8 us
    pallas_call x1, Pallas kernels, shards(): pl.pallas_call(grid_kernel, out_shape=jax.ShapeDtypeStruct((128 * ROWS_BA...  6.16 us
    pallas_call x1, Pallas kernels, shards(): pl.pallas_call(send_kernel, out_shape=(jax.ShapeDtypeStruct((128 * ROWS_O...  3.79 us
    pallas_call x1, Pallas kernels, shards(): pl.pallas_call(update_kernel, out_shape=jax.ShapeDtypeStruct((8, 512, 128...  3.27 us

profile of v6, /device:TPU:0, one launch (start us, length us, event | category | flops | bytes accessed | tf_op | source)
XLA Modules:
  0.0 106.9 jit_solution(9129397408717210820)
XLA Ops:
  0.0 3.8 %send.1 = (f32[6144,128]{1,0:T(8,128)S(1)}, f32[8,128]{1,0:T(8,128)S(1)}, f32[7,4,64,256]{3,2,1,0:T(8,128)S(1)}) custom-call(s32[3]{0:T(128)} %cutoffs_far.1, f32[8]{0:T(128)} %damping_far.1, f32[8]{0:T(128)} %power_far.1, s32[1,256]{1,0:T(1,128)} %bitcast.19, f32[8,512,128]{2,1,0:T(8,128)} %bitcast.16, bf16[512,256]{1,0:T(8,128)(2,1)} %constant.20.clone.w_high_far, ...), custom_call_target="tpu_custom_call" | custom-call | tf_op jit(solution)/shard_map/send/pallas_call | solution.py:530
  3.8 0.0 copy-start.3
  3.8 0.0 copy-start.4
  3.8 0.0 copy-start.5
  3.8 0.0 copy-start.6
  3.8 0.0 copy-start.7
  3.9 0.0 copy-start.8
  3.9 0.0 copy-start.9
  3.9 52.7 %all_to_all.10.came = f32[128,48,128]{2,1,0:T(8,128)S(1)} all-to-all(f32[128,48,128]{2,1,0:T(8,128)S(1)} %bitcast.18), channel_id=1, replica_groups=mesh['grp'=4,'slab_0'=4,'slab_1'=4,'slab_2'=2] {'grp','slab_0','slab_1',..., dimensions={0} | all-to-all | bytes 6291456 | tf_op jit(solution)/shard_map/all_to_all | solution.py:553
  56.5 0.0 copy-done.3
  56.5 0.0 copy-done.4
  56.6 0.0 copy-done.5
  56.6 0.0 copy-done.6
  56.6 0.0 copy-done.7
  56.6 0.0 copy-done.8
  56.6 0.0 copy-done.9
  56.6 6.2 %grid.1 = f32[5248,128]{1,0:T(8,128)S(1)} custom-call(f32[128,48,128]{2,1,0:T(8,128)S(1)} %all_to_all.10.came, f32[8,128]{1,0:T(8,128)S(1)} %get-tuple-element.9.sums, s32[1,256]{1,0:T(1,128)S(1)} %bitcast.20, bf16[256,256]{1,0:T(8,128)(2,1)S(1)} %copy-done.6, bf16[256,256]{1,0:T(8,128)(2,1)S(1)} %copy-done.5, bf16[256,256]{1,0:T(8,128)(2,1)S(1)} %copy-done.4, ...), custom_call_target="tpu_custom_call" | custom-call | tf_op jit(solution)/shard_map/grid/pallas_call | solution.py:555
  62.8 0.0 copy-start
  62.8 0.0 copy-start.1
  62.8 0.0 copy-start.2
  62.8 40.8 %all_to_all.11 = f32[128,1,5248]{2,1,0:T(1,128)S(1)} all-to-all(f32[128,1,5248]{2,1,0:T(1,128)S(1)} %bitcast.14), channel_id=1, replica_groups=mesh['grp'=4,'slab_0'=4,'slab_1'=4,'slab_2'=2] {'grp','slab_0','slab_1',..., dimensions={0} | all-to-all | bytes 5373952 | tf_op jit(solution)/shard_map/all_to_all | solution.py:570
  103.6 0.0 copy-done
  103.6 0.0 copy-done.1
  103.6 0.0 copy-done.2
  103.6 3.3 %update.1 = f32[8,512,128]{2,1,0:T(8,128)} custom-call(f32[5248,128]{1,0:T(8,128)S(1)} %bitcast.15, f32[8,512,128]{2,1,0:T(8,128)S(1)} %bitcast.17, f32[7,4,64,256]{3,2,1,0:T(8,128)S(1)} %get-tuple-element.10.factors, bf16[256,256]{1,0:T(8,128)(2,1)S(1)} %copy-done.2, bf16[256,256]{1,0:T(8,128)(2,1)S(1)} %copy-done.1), custom_call_target="tpu_custom_call" | custom-call | tf_op jit(solution)/shard_map/update/pallas_call | solution.py:572
Async XLA Ops:
  3.8 52.8 %copy-start.3 = (bf16[256,256]{1,0:T(8,128)(2,1)S(1)}, bf16[256,256]{1,0:T(8,128)(2,1)}, u32[]{:S(2)}) copy-start(bf16[256,256]{1,0:T(8,128)(2,1)} %constant.25.clone.xi_low) | copy-start | bytes 393220
  3.8 52.7 %copy-start.4 = (bf16[256,256]{1,0:T(8,128)(2,1)S(1)}, bf16[256,256]{1,0:T(8,128)(2,1)}, u32[]{:S(2)}) copy-start(bf16[256,256]{1,0:T(8,128)(2,1)} %constant.24.clone.xi_high) | copy-start | bytes 393220
  3.8 52.7 %copy-start.5 = (bf16[256,256]{1,0:T(8,128)(2,1)S(1)}, bf16[256,256]{1,0:T(8,128)(2,1)}, u32[]{:S(2)}) copy-start(bf16[256,256]{1,0:T(8,128)(2,1)} %constant.23.clone.zt_low) | copy-start | bytes 393220
  3.8 52.7 %copy-start.6 = (bf16[256,256]{1,0:T(8,128)(2,1)S(1)}, bf16[256,256]{1,0:T(8,128)(2,1)}, u32[]{:S(2)}) copy-start(bf16[256,256]{1,0:T(8,128)(2,1)} %constant.22.clone.zt_high) | copy-start | bytes 393220
  3.8 52.7 %copy-start.7 = (bf16[176,256]{1,0:T(8,128)(2,1)S(1)}, bf16[176,256]{1,0:T(8,128)(2,1)}, u32[]{:S(2)}) copy-start(bf16[176,256]{1,0:T(8,128)(2,1)} %constant.27.clone.xf_low) | copy-start | bytes 270340
  3.9 52.7 %copy-start.8 = (bf16[176,256]{1,0:T(8,128)(2,1)S(1)}, bf16[176,256]{1,0:T(8,128)(2,1)}, u32[]{:S(2)}) copy-start(bf16[176,256]{1,0:T(8,128)(2,1)} %constant.26.clone.xf_high) | copy-start | bytes 270340
  3.9 52.7 %copy-start.9 = (s32[256]{0:T(256)S(1)}, s32[256]{0:T(256)}, u32[]{:S(2)}) copy-start(s32[256]{0:T(256)} %param.16) | copy-start | bytes 3076
  62.8 40.9 %copy-start = (f32[4,2,64,4,256]{4,3,2,1,0:T(4,128)S(1)}, f32[4,2,64,4,256]{4,3,2,1,0:T(4,128)}, u32[]{:S(2)}) copy-start(f32[4,2,64,4,256]{4,3,2,1,0:T(4,128)} %param.15) | copy-start | bytes 6291460
  62.8 40.8 %copy-start.1 = (bf16[256,256]{1,0:T(8,128)(2,1)S(1)}, bf16[256,256]{1,0:T(8,128)(2,1)}, u32[]{:S(2)}) copy-start(bf16[256,256]{1,0:T(8,128)(2,1)} %constant.29.clone.yf_low) | copy-start | bytes 393220
  62.8 40.8 %copy-start.2 = (bf16[256,256]{1,0:T(8,128)(2,1)S(1)}, bf16[256,256]{1,0:T(8,128)(2,1)}, u32[]{:S(2)}) copy-start(bf16[256,256]{1,0:T(8,128)(2,1)} %constant.28.clone.yf_high) | copy-start | bytes 393220
